TPU v7x, 32 devices: a whole 2x2x4 slice. The times are simulated.
32 devices in a mesh: dp: 8 (over z, y), tensor: 4 (over x, core).
Axes of the slice: x: 2, y: 2, z: 4, core: 2. Of those that a mesh axis runs over, the one named last changes fastest.
Arguments:
- tokens: int32 [16384], P('dp'), may hold values from 0 to 8190
- lengths: int32 [16, 4], P('dp'), may hold values from 1 to 512, 1024 in all within a row
- timesteps: int32 [16], P('dp'), may hold values from 1 to 1000, as said below
- masks: int32 [16384], P('dp'), may hold values from 0 to 1, as said below
- step_count: int32 [1], replicated, may hold values from 2 to 20
- table: float32 [8192, 768], P('tensor', 'dp'), may hold values from -0.4375 to 0.4375
- joint_weight: float32 [768, 2304], P('dp', 'tensor'), may hold values from -0.21875 to 0.21875
- output_weight: float32 [768, 768], P('tensor', 'dp'), may hold values from -1.75 to 1.75
- upward_weight: float32 [768, 3072], P('dp', 'tensor'), may hold values from -0.21875 to 0.21875
- downward_weight: float32 [3072, 768], P('tensor', 'dp'), may hold values from -0.21875 to 0.21875
- gains: float32 [3, 768], P(None, 'dp'), may hold values from 0.5 to 1.5
- momentum_table: float32 [8192, 768], P('tensor', 'dp'), may hold values from -3.8146973e-06 to 3.8146973e-06
- momentum_joint: float32 [768, 2304], P('dp', 'tensor'), may hold values from -3.8146973e-06 to 3.8146973e-06
- momentum_output: float32 [768, 768], P('tensor', 'dp'), may hold values from -3.8146973e-06 to 3.8146973e-06
- momentum_upward: float32 [768, 3072], P('dp', 'tensor'), may hold values from -3.8146973e-06 to 3.8146973e-06
- momentum_downward: float32 [3072, 768], P('tensor', 'dp'), may hold values from -3.8146973e-06 to 3.8146973e-06
- momentum_gains: float32 [3, 768], P(None, 'dp'), may hold values from -1.9073486e-05 to 1.9073486e-05
- variance_table: float32 [8192, 768], P('tensor', 'dp'), may hold values from 2.9919196e-14 to 1.1967678e-13
- variance_joint: float32 [768, 2304], P('dp', 'tensor'), may hold values from 2.9919196e-14 to 1.1967678e-13
- variance_output: float32 [768, 768], P('tensor', 'dp'), may hold values from 2.9919196e-14 to 1.1967678e-13
- variance_upward: float32 [768, 3072], P('dp', 'tensor'), may hold values from 2.9919196e-14 to 1.1967678e-13
- variance_downward: float32 [3072, 768], P('tensor', 'dp'), may hold values from 2.9919196e-14 to 1.1967678e-13
- variance_gains: float32 [3, 768], P(None, 'dp'), may hold values from 7.4797986e-13 to 2.9919194e-12
Outputs:
- loss: float32 [], replicated
- grad_norm: float32 [], replicated
- new_momentum_table: float32 [8192, 768], P('tensor', 'dp')
- new_variance_table: float32 [8192, 768], P('tensor', 'dp')
- new_table: float32 [8192, 768], P('tensor', 'dp')
- new_momentum_joint: float32 [768, 2304], P('dp', 'tensor')
- new_variance_joint: float32 [768, 2304], P('dp', 'tensor')
- new_joint: float32 [768, 2304], P('dp', 'tensor')
- new_momentum_output: float32 [768, 768], P('tensor', 'dp')
- new_variance_output: float32 [768, 768], P('tensor', 'dp')
- new_output: float32 [768, 768], P('tensor', 'dp')
- new_momentum_upward: float32 [768, 3072], P('dp', 'tensor')
- new_variance_upward: float32 [768, 3072], P('dp', 'tensor')
- new_upward: float32 [768, 3072], P('dp', 'tensor')
- new_momentum_downward: float32 [3072, 768], P('tensor', 'dp')
- new_variance_downward: float32 [3072, 768], P('tensor', 'dp')
- new_downward: float32 [3072, 768], P('tensor', 'dp')
- new_momentum_gains: float32 [3, 768], P(None, 'dp')
- new_variance_gains: float32 [3, 768], P(None, 'dp')
- new_gains: float32 [3, 768], P(None, 'dp')
Inputs may be any that keep to these rules, and one draw needn't show every extreme that they name: `timesteps`: a sequence's timestep is drawn uniformly; some sequence has timestep 1 and some has 1000. `masks`: each position of sequence s is masked independently with probability timesteps[s] / 1000.
All inputs are finite; a program needn't handle non-finite values.
Results may differ from a plain program's by a relative error of at most 0.0082.
Values may be sent and summed in bfloat16 or wider, within the bound.
A program may use at most 192 MiB of HBM per device.

v0:
```python
import functools

import jax
import jax.numpy as jnp
from jax import lax
from jax.experimental import pallas as pl
from jax.experimental.pallas import tpu as pltpu
from jax.sharding import PartitionSpec as P

D = 768
HEAD_DIM = 64
VOCAB = 8192
SEQ_LEN = 1024
DOCS = 4
T_DIFF = 1000


eps_norm = 1e-06
neg_fill = -1000000000.0
beta_one = 0.9
beta_two = 0.999
adam_eps = 1e-08
clip_at = 0.02
rates = (0.05, 0.03, 0.25, 0.03, 0.03, 0.3)
decays = (0.1, 0.1, 0.1, 0.1, 0.1, 0.0)


def norm_apply(values, gain):
    inverse = lax.rsqrt(jnp.mean(values * values, axis=-1, keepdims=True) + eps_norm)
    return values * inverse * gain


def norm_back(values, gain, upstream):
    inverse = lax.rsqrt(jnp.mean(values * values, axis=-1, keepdims=True) + eps_norm)
    gain_grad = jnp.sum(upstream * values * inverse, axis=0)
    scaled = upstream * gain
    inner = jnp.mean(scaled * values, axis=-1, keepdims=True)
    return (inverse * (scaled - values * inverse * inverse * inner), gain_grad)


def rotate(values, cosine, sine):
    middle = values.shape[-1] // 2
    front_part = values[..., :middle]
    back_part = values[..., middle:]
    return jnp.concatenate(
        [front_part * cosine - back_part * sine, back_part * cosine + front_part * sine], axis=-1
    )


def groups_of(count):
    groups, bit, width = [], 1, 1
    while bit < count:
        masks = [bit]
        if width == 2 and bit * 2 < count:
            masks = [bit, 2 * bit, 3 * bit]
            bit = bit * 2
        groups.append(masks)
        bit, width = bit * 2, 2
    return groups


def swap(value, axis, mask):
    size = lax.axis_size(axis)
    return lax.ppermute(value, axis, [(place, place ^ mask) for place in range(size)])


def spread(value, masks):
    return jnp.concatenate([value] + [swap(value, "dp", mask) for mask in masks], axis=0)


def gather_all(value, x_last):
    groups = groups_of(lax.axis_size("dp"))
    for masks in groups[:0:-1]:
        value = spread(value, masks)
    if x_last:
        value = spread(value, groups[0])
        other = swap(value, "tensor", 2)
    else:
        other = swap(value, "tensor", 2)
        value = spread(value, groups[0])
        other = spread(other, groups[0])
    return [value, other, swap(value, "tensor", 1), swap(other, "tensor", 1)]


MESH = pl.DeviceIdType.MESH


def neighbours():
    column, row = lax.axis_index("dp"), lax.axis_index("tensor")
    return {
        "x": (column, (row + 2) % 4),
        "c": (column, row + 1 - 2 * (row % 2)),
        "y": (column + 1 - 2 * (column % 2), row),
        "up": (column + 2, row),
        "down": (column - 2, row),
    }


def meet(z, devices):
    barrier = pltpu.get_barrier_semaphore()

    def greet(name):
        pl.semaphore_signal(barrier, inc=1, device_id=devices[name], device_id_type=MESH)

    for name in ("x", "c", "y"):
        greet(name)
    pl.when(z < 3)(lambda: greet("up"))
    pl.when(z > 0)(lambda: greet("down"))
    pl.semaphore_wait(barrier, 3 + (z + 2) // 3 + (5 - z) // 3)


def start_body(items, *refs):
    ins = refs[:items]
    places, cosine, sine, seg_row, seg_col = refs[items : items + 5]
    refs = refs[items + 5 :]
    outs = [refs[4 * item : 4 * item + 4] for item in range(items)]
    embedded_out, normed, packed, lse, attended = refs[4 * items : 4 * items + 5]
    refs = refs[4 * items + 5 :]
    side_sem, z_sem, recv_sem, own_sem, keep_sem = refs[:5]
    staged = refs[5:7]
    attend_refs = refs[7:]
    column = lax.axis_index("dp")
    z = column // 2
    devices = neighbours()
    meet(z, devices)
    shard = [item.shape[0] for item in ins]
    piece = [item // 2 for item in shard]

    def base(item, quarter):
        return staged[item].at[quarter] if item < 2 else outs[item][quarter]

    def mirror(source):
        return source + 1 - 2 * (source % 2)

    def view(item, part, quarter, source):
        start = pl.multiple_of(source * shard[item] + part * piece[item], 8)
        return base(item, quarter).at[pl.ds(start, piece[item])]

    def copy(item, part, quarter, source, to_quarter, name, send, own=False):
        here = view(item, part, quarter, source)
        if own:
            here = ins[item].at[pl.ds(part * piece[item], piece[item])]
        return pltpu.make_async_remote_copy(
            src_ref=here,
            dst_ref=view(item, part, to_quarter, source),
            send_sem=send,
            recv_sem=recv_sem.at[item, part, to_quarter, source],
            device_id=devices[name],
            device_id_type=MESH,
        )

    def arrived(item, part, quarter, source):
        copy(item, part, quarter, source, quarter, "x", side_sem.at[0, item]).wait_recv()

    def send_x(item, part, source, own=False):
        copy(item, part, 0, source, 2, "x", side_sem.at[0, item], own).start()

    def send_y(item, part, quarter, source, own=False):
        copy(item, part, quarter, source, quarter, "y", side_sem.at[1, item], own).start()

    def send_c(item, part, quarter, source, own=False):
        copy(item, part, quarter, source, quarter + 1, "c", side_sem.at[2 + quarter // 2, item], own).start()

    def send_z(item, part, source, turn, upward, own=False):
        name = "up" if upward else "down"
        copy(item, part, 0, source, 0, name, z_sem.at[item, part, 1 - upward, turn], own).start()

    def slot(turn, action):
        pl.when(z >= turn)(lambda: action(column - 2 * turn, 1))
        pl.when(z + turn <= 3)(lambda: action(column + 2 * turn, 0))

    every = [(item, part) for item in range(items) for part in range(2)]

    def local(item):
        return pltpu.make_async_copy(
            ins[item],
            base(item, 0).at[pl.ds(pl.multiple_of(column * shard[item], 8), shard[item])],
            own_sem.at[item],
        )

    def keep(item, quarter):
        return pltpu.make_async_copy(staged[item].at[quarter], outs[item][quarter], keep_sem.at[item, quarter])

    def begin(item):
        for part in range(2):
            pl.when(z < 3)(lambda: send_z(item, part, column, 0, 1, True))
            pl.when(z > 0)(lambda: send_z(item, part, column, 0, 0, True))
            send_x(item, part, column, True)
            send_y(item, part, 0, column, True)
            send_c(item, part, 0, column, True)
        local(item).start()

    def from_z(item, part, turn, source, upward):
        arrived(item, part, 0, source)
        if turn < 3:
            ahead = z < 3 if upward else z > 0
            pl.when(ahead)(lambda: send_z(item, part, source, turn, upward))
        send_x(item, part, source)
        send_y(item, part, 0, source)
        send_c(item, part, 0, source)

    def second(item, source):
        arrived(item, 0, 0, mirror(source))
        send_x(item, 0, mirror(source))
        send_c(item, 0, 0, mirror(source))
        arrived(item, 1, 2, source)
        send_y(item, 1, 2, source)
        send_c(item, 1, 2, source)

    def third(item, source):
        arrived(item, 0, 2, source)
        send_c(item, 0, 2, source)
        arrived(item, 1, 0, mirror(source))
        send_c(item, 1, 0, mirror(source))
        for part in range(2):
            arrived(item, part, 2, mirror(source))
            send_c(item, part, 2, mirror(source))

    def along_z(item, turn):
        for part in range(2):
            slot(turn, lambda source, upward: from_z(item, part, turn, source, upward))

    def onward(action, item, turn):
        if turn == 0:
            action(item, column)
        else:
            slot(turn, lambda source, upward: action(item, source))

    def complete(item):
        for part in range(2):
            for source in range(8):
                for quarter in (1, 3):
                    arrived(item, part, quarter, source)
        local(item).wait()
        if item < 2:
            for quarter in range(4):
                keep(item, quarter).start()

    rest = range(2, items)
    begin(0)
    for turn in (1, 2, 3):
        along_z(0, turn)
    begin(1)
    for turn in range(4):
        onward(second, 0, turn)
    for turn in (1, 2, 3):
        along_z(1, turn)
    for turn in range(4):
        onward(third, 0, turn)
    for item in rest:
        begin(item)
    complete(0)

    def look_up(quarter):
        def one(chunk, _):
            at = pl.ds(pl.multiple_of(chunk * 512, 512), 512)
            spots = lax.broadcasted_iota(jnp.int32, (places.shape[0], 512), 1) + chunk * 512
            hot = jnp.where(places[:, quarter : quarter + 1] == spots, 1.0, 0.0).astype(jnp.bfloat16)
            embedded_out[...] += lax.dot_general(
                hot, staged[0][quarter, :, at], (((1,), (1,)), ((), ())), preferred_element_type=jnp.float32
            )
            return 0

        lax.fori_loop(0, staged[0].shape[2] // 512, one, 0)

    embedded_out[...] = jnp.zeros_like(embedded_out)
    look_up(0)
    for turn in range(4):
        onward(second, 1, turn)
    look_up(2)
    for item in rest:
        along_z(item, 1)
    look_up(1)
    for turn in range(4):
        onward(third, 1, turn)
    for item in rest:
        along_z(item, 2)
    look_up(3)
    complete(1)
    gain = staged[1][0, :, 512:640].astype(jnp.float32).T[64:65]
    value = embedded_out[...] * D**0.5
    embedded_out[...] = value
    inverse = lax.rsqrt(jnp.mean(value * value, axis=-1, keepdims=True) + eps_norm)
    normed[...] = (value * inverse * gain).astype(jnp.bfloat16)
    for item in rest:
        along_z(item, 3)

    def between(stage):
        for item in rest:
            if stage == 0:
                onward(second, item, 0)
                onward(second, item, 1)
            if stage == 1:
                onward(second, item, 2)
                onward(second, item, 3)
            if stage in (3, 4, 5):
                onward(third, item, (0, 1, 2)[stage - 3])
            if stage == 6:
                onward(third, item, 3)

    attend_steps(
        normed, [staged[1].at[q] for q in range(4)], cosine, sine, seg_row, seg_col, packed, lse, attended, between, *attend_refs
    )
    for item in rest:
        complete(item)
    for item in range(2):
        for quarter in range(4):
            keep(item, quarter).wait()
    for item in range(items):
        for way, count in enumerate((12, 12, 16, 16)):
            lead = base(item, 0).at[pl.ds(0, count * piece[item])]
            pltpu.make_async_remote_copy(
                src_ref=lead,
                dst_ref=lead,
                send_sem=side_sem.at[way, item],
                recv_sem=recv_sem.at[item, 0, 0, 0],
                device_id=devices["x"],
                device_id_type=MESH,
            ).wait_send()
    for item, part in every:
        for turn in range(3):
            pl.when((z < 3) & (z >= turn))(
                lambda: copy(item, part, 0, column, 0, "up", z_sem.at[item, part, 0, turn], True).wait_send()
            )
            pl.when((z > 0) & (z + turn <= 3))(
                lambda: copy(item, part, 0, column, 0, "down", z_sem.at[item, part, 1, turn], True).wait_send()
            )


def start_kernel(shards, places, cosine, sine, seg_row, seg_col):
    items = len(shards)
    anywhere = pl.BlockSpec(memory_space=pl.ANY)
    inside = pl.BlockSpec(memory_space=pltpu.VMEM)
    whole, rows = lax.axis_size("dp"), places.shape[0]
    full = [(item.shape[0] * whole, item.shape[1]) for item in shards]
    shapes = [jax.ShapeDtypeStruct(shape, jnp.bfloat16) for shape in full for _ in range(4)]
    flat = pl.pallas_call(
        functools.partial(start_body, items),
        name="start",
        out_shape=shapes
        + [
            jax.ShapeDtypeStruct((rows, full[0][0]), jnp.float32),
            jax.ShapeDtypeStruct((rows, full[0][0]), jnp.bfloat16),
            jax.ShapeDtypeStruct((6, 2 * rows, 256), jnp.bfloat16),
            jax.ShapeDtypeStruct((8, 2 * rows), jnp.float32),
            jax.ShapeDtypeStruct((rows, 768), jnp.bfloat16),
        ],
        in_specs=[anywhere] * items + [inside] * 5,
        out_specs=[anywhere] * (4 * items) + [inside] * 5,
        scratch_shapes=[
            pltpu.SemaphoreType.DMA((4, items)),
            pltpu.SemaphoreType.DMA((items, 2, 2, 3)),
            pltpu.SemaphoreType.DMA((items, 2, 4, 8)),
            pltpu.SemaphoreType.DMA((items,)),
            pltpu.SemaphoreType.DMA((2, 4)),
            pltpu.VMEM((4, *full[0]), jnp.bfloat16),
            pltpu.VMEM((4, *full[1]), jnp.bfloat16),
            pltpu.VMEM((6, rows, 256), jnp.bfloat16),
            pltpu.VMEM((6, 2 * rows, 128), jnp.bfloat16),
            pltpu.VMEM((6, rows, 128), jnp.bfloat16),
            pltpu.SemaphoreType.DMA((6,)),
            pltpu.SemaphoreType.DMA((6,)),
            pltpu.SemaphoreType.DMA((6,)),
            pltpu.SemaphoreType.DMA((6,)),
        ],
        compiler_params=pltpu.CompilerParams(
            collective_id=0, has_side_effects=True, vmem_limit_bytes=56 << 20
        ),
    )(*shards, places, cosine, sine, seg_row, seg_col)
    return [flat[4 * item : 4 * item + 4] for item in range(items)], flat[4 * items :]


def reduce_body(layout, parts, gains_at, *refs):
    items = len(layout)
    wide_refs = [refs[4 * item : 4 * item + 4] for item in range(items)]
    refs = refs[4 * items :]
    facts, places, extra = refs[:3]
    lefts = refs[3:9]
    refs = refs[9:]
    outs, totals = refs[:items], refs[items]
    refs = refs[items + 1 :]
    held = [refs[6 * item : 6 * item + 6] for item in range(items)]
    refs = refs[6 * items :]
    side_sem, c_send, c_sem, x_sem, y_sem, zs_sem, zr_sem, load_sem, free_sem = refs[:9]
    tile, tile_row, tile_column, row_send, row_recv, column_send, column_recv = refs[9:16]
    crossed, from_c, rights = refs[16:]
    column = lax.axis_index("dp")
    z, y = column // 2, column % 2
    devices = neighbours()
    shard = [item.shape[0] for item in outs]
    piece = [item // 2 for item in shard]
    width = [item.shape[1] for item in outs]

    def load(item, quarter):
        return pltpu.make_async_copy(
            wide_refs[item][quarter],
            rights.at[quarter, :, pl.ds(0, width[item])],
            load_sem.at[item, quarter],
        )

    for quarter in range(4):
        load(0, quarter).start()
    row = lax.axis_index("tensor")
    row_peers = [(column, (row + away) % 4) for away in (1, 2, 3)]
    column_peers = [((column + away) % 8, row) for away in range(1, 8)]
    barrier = pltpu.get_barrier_semaphore()
    for device in row_peers + column_peers:
        pl.semaphore_signal(barrier, inc=1, device_id=device, device_id_type=MESH)
    pl.semaphore_wait(barrier, 10)

    def span(item, part, source):
        return pl.ds(pl.multiple_of(source * shard[item] + part * piece[item], 8), piece[item])

    def remote(src, dst, send, recv, name):
        return pltpu.make_async_remote_copy(
            src_ref=src, dst_ref=dst, send_sem=send, recv_sem=recv, device_id=devices[name], device_id_type=MESH
        )

    def c_copy(item, part, side, source, slot=0):
        here = pl.ds(pl.multiple_of(source % 2 * shard[item] + part * piece[item], 8), piece[item])
        columns = pl.ds(0, width[item])
        return remote(
            crossed.at[side, slot, here, columns],
            from_c.at[side, span(item, part, source), columns],
            c_send.at[side, slot],
            c_sem.at[item, part, side, source],
            "c",
        )

    def c_wait(item, part, side, source):
        c_copy(item, part, side, source).wait_recv()

    def c_sent(item, slot):
        for side in range(2):
            lead = crossed.at[side, slot, :, pl.ds(0, width[item])]
            remote(lead, lead, c_send.at[side, slot], c_sem.at[0, 0, 0, 0], "c").wait_send()

    def x_copy(item, part, source):
        place = source if part == 0 else source // 2
        return remote(
            held[item][0].at[1, span(item, part, source)],
            held[item][1 + part].at[place],
            side_sem.at[0, item],
            x_sem.at[item, part, place],
            "x",
        )

    def y_copy(item, part, side, source):
        return remote(
            held[item][0].at[side, span(item, part, source)],
            held[item][3].at[source // 2] if part == 0 else held[item][4].at[side, source // 2],
            side_sem.at[1, item],
            y_sem.at[item, part + side, source // 2],
            "y",
        )

    def z_copy(item, part, source, away, upward):
        return remote(
            held[item][0].at[0, span(item, part, source)],
            held[item][5].at[1 - upward, part, away],
            zs_sem.at[item, part, 1 - upward, away],
            zr_sem.at[item, part, 1 - upward, away],
            "up" if upward else "down",
        )

    def add(item, side, part, source, *others):
        total = held[item][0]
        start = source * shard[item] + part * piece[item]
        step = 16

        def one(turn, _):
            here = pl.ds(pl.multiple_of(start + turn * step, 8), step)
            value = total[side, here].astype(jnp.float32)
            for other in others:
                value = value + other(turn * step, step)
            total[side, here] = value.astype(jnp.bfloat16)
            return 0

        lax.fori_loop(0, piece[item] // step, one, 0)

    def c_part(item, side, part, source):
        start = source * shard[item] + part * piece[item]

        def read(at, step):
            here = pl.ds(pl.multiple_of(start + at, 8), step)
            return from_c[side, here, pl.ds(0, width[item])].astype(jnp.float32)

        return read

    def of(ref, *place):
        return lambda at, step: ref[(*place, pl.ds(pl.multiple_of(at, 8), step))].astype(jnp.float32)

    def mirror(source):
        return source + 1 - 2 * (source % 2)

    def target(turn):
        low = 3 - turn if turn < 2 else jnp.where(z % 3 == 0, 3 - turn, turn - 2)
        return column + 2 * (jnp.where(z < 2, low, 3 - low) - z)

    def send_c(item, turn):
        source = target(turn)
        if item > 0:
            pl.semaphore_wait(free_sem, 1)
        for part, side, place in (
            (0, 1, source),
            (1, 1, mirror(source)),
            (0, 1, mirror(source)),
            (1, 0, mirror(source)),
            (0, 0, mirror(source)),
            (1, 1, source),
            (0, 0, source),
            (1, 0, source),
        ):
            c_copy(item, part, side, place, turn % 2).start()

    def make(item, turn):
        if 4 * item + turn >= 2:
            c_sent(item if turn >= 2 else item - 1, turn % 2)
        block = 2 * shard[item]
        rows = pl.ds(pl.multiple_of(target(turn) // 2 * block, 16), block)
        for quarter in range(4):
            if turn == 0:
                load(item, quarter).wait()
            for left, base, span_width, step in layout[item]:

                def one(chunk, _):
                    at = pl.ds(pl.multiple_of(base + chunk * step, 128), step)
                    found = jnp.dot(
                        lefts[left][rows], rights[quarter, :, at], preferred_element_type=jnp.float32
                    )
                    if item == 0:
                        spots = lax.broadcasted_iota(jnp.int32, (places.shape[0], step), 1) + chunk * step
                        hot = jnp.where(places[:, quarter : quarter + 1] == spots, 1.0, 0.0)
                        found += jnp.dot(
                            lefts[1][rows], hot.astype(jnp.bfloat16), preferred_element_type=jnp.float32
                        )
                    if item == gains_at[0] and base == 0:
                        found += extra[rows]
                    if quarter % 2:
                        crossed[quarter // 2, turn % 2, :, at] = found.astype(jnp.bfloat16)
                    else:
                        held[item][0][quarter // 2, rows, at] = found.astype(jnp.bfloat16)
                    return 0

                lax.fori_loop(0, span_width // step, one, 0)
        if turn == 3 and item + 1 < items:
            for quarter in range(4):
                load(item + 1, quarter).start()

    def first(item, turn):
        source = target(turn)
        for x_place, y_side in ((source, 1), (mirror(source), 0)):
            c_wait(item, 0, 1, x_place)
            add(item, 1, 0, x_place, c_part(item, 1, 0, x_place))
            x_copy(item, 0, x_place).start()
            y_place = mirror(source)
            c_wait(item, 1, y_side, y_place)
            add(item, y_side, 1, y_place, c_part(item, y_side, 1, y_place))
            y_copy(item, 1, y_side, y_place).start()

    def second(item, turn):
        source = target(turn)
        place = mirror(source)
        c_wait(item, 0, 0, place)
        x_copy(item, 0, place).wait_recv()
        add(item, 0, 0, place, c_part(item, 0, 0, place), of(held[item][1], place))
        y_copy(item, 0, 0, place).start()
        c_wait(item, 1, 1, source)
        y_copy(item, 1, 1, source).wait_recv()
        add(item, 1, 1, source, c_part(item, 1, 1, source), of(held[item][4], 1, source // 2))
        x_copy(item, 1, source).start()

    def third(item, turn):
        source = target(turn)
        for part in range(2):
            c_wait(item, part, 0, source)
            x_copy(item, part, source).wait_recv()
            y_copy(item, part, 0, source).wait_recv()
            if part == 0:
                terms = [of(held[item][1], source), of(held[item][3], source // 2)]
            else:
                terms = [of(held[item][2], source // 2), of(held[item][4], 0, source // 2)]
            add(item, 0, part, source, c_part(item, 0, part, source), *terms)
        if item + 1 < items:
            pl.semaphore_signal(free_sem, inc=1, device_id=devices["c"], device_id_type=MESH)

    def fourth(item, turn):
        source = target(turn)
        away = jnp.where(source > column, source - column, column - source) // 2

        def along(upward):
            for part in range(2):

                def more():
                    z_copy(item, part, source, away, upward).wait_recv()
                    add(item, 0, part, source, of(held[item][5], 1 - upward, part, away))

                pl.when(z > 0 if upward else z < 3)(more)
                z_copy(item, part, source, away - 1, upward).start()

        pl.when(source > column)(lambda: along(1))
        pl.when(source < column)(lambda: along(0))

    def last(item):
        square = jnp.zeros((), jnp.float32)
        for part in range(2):
            for upward in (1, 0):
                pl.when(z > 0 if upward else z < 3)(
                    lambda: z_copy(item, part, column, 0, upward).wait_recv()
                )
            start = column * shard[item] + part * piece[item]

            def one(turn, square):
                at = pl.multiple_of(turn * 16, 8)
                value = held[item][0][0, pl.ds(pl.multiple_of(start + at, 8), 16)].astype(jnp.float32)
                below = held[item][5][0, part, 0, pl.ds(at, 16)].astype(jnp.float32)
                above = held[item][5][1, part, 0, pl.ds(at, 16)].astype(jnp.float32)
                value = value + jnp.where(z > 0, below, 0.0) + jnp.where(z < 3, above, 0.0)
                outs[item][pl.ds(pl.multiple_of(part * piece[item] + at, 8), 16)] = value
                square_here = value * value
                if item == gains_at[0]:
                    lane = lax.broadcasted_iota(jnp.int32, value.shape, 1)
                    repeated = (lane >= gains_at[1]) & (lane < gains_at[1] + gains_at[2])
                    square_here = jnp.where(repeated, square_here / parts, square_here)
                return square + jnp.sum(square_here)

            square = lax.fori_loop(0, piece[item] // 16, one, square)
        return square

    steps = [(item, turn) for item in range(items) for turn in range(4)]
    count = len(steps)
    make(*steps[0])
    send_c(*steps[0])
    for turn in range(count + 3):
        if turn < count:
            first(*steps[turn])
        if turn + 1 < count:
            make(*steps[turn + 1])
            send_c(*steps[turn + 1])
        if 0 <= turn - 1 < count:
            second(*steps[turn - 1])
        if 0 <= turn - 2 < count:
            third(*steps[turn - 2])
        if 0 <= turn - 3 < count and (turn - 3) % 4 < 3:
            fourth(*steps[turn - 3])
    square = sum([last(item) for item in range(items)])
    sublane = lax.broadcasted_iota(jnp.int32, (8, 128), 0)
    tile[...] = jnp.where(sublane == 0, square, facts[...])

    def exchange(value, slots, here, peers, sources, send, recv):
        slots[here] = value

        def crossing(place, device, source):
            return pltpu.make_async_remote_copy(
                src_ref=slots.at[here],
                dst_ref=slots.at[source],
                send_sem=send.at[place],
                recv_sem=recv.at[source],
                device_id=device,
                device_id_type=MESH,
            )

        for place, device in enumerate(peers):
            crossing(place, device, here).start()
        for place, device in enumerate(peers):
            crossing(place, device, sources[place]).wait_recv()
        total = slots[0]
        for place in range(1, len(peers) + 1):
            total = total + slots[place]
        for place, device in enumerate(peers):
            crossing(place, device, here).wait_send()
        return total

    along_row = exchange(
        tile[...], tile_row, row, row_peers, [(row + away) % 4 for away in (1, 2, 3)], row_send, row_recv
    )
    totals[...] = exchange(
        along_row,
        tile_column,
        column,
        column_peers,
        [(column + away) % 8 for away in range(1, 8)],
        column_send,
        column_recv,
    )
    for slot in range(2):
        c_sent(items - 1, slot)
    for item in range(items):
        for way, count in enumerate((12, 12)):
            lead = held[item][0].at[0, pl.ds(0, count * piece[item])]
            remote(lead, lead, side_sem.at[way, item], c_sem.at[item, 0, 0, 0], "x").wait_send()
        for part in range(2):
            for away in range(3):
                pl.when((z < 3) & (z + away + 1 <= 3))(
                    lambda: z_copy(item, part, column, away, 1).wait_send()
                )
                pl.when((z > 0) & (z - away - 1 >= 0))(
                    lambda: z_copy(item, part, column, away, 0).wait_send()
                )


def reduce_kernel(layout, lefts, rights, places, extra, facts, parts, gains_at, tag):
    items = len(layout)
    anywhere = pl.BlockSpec(memory_space=pl.ANY)
    inside = pl.BlockSpec(memory_space=pltpu.VMEM)
    whole = lax.axis_size("dp")
    rows, depth = lefts[0].shape
    half = rows // (2 * whole)
    widths = [item[0].shape[1] for item in rights]
    shapes, scratch = [], []
    for width in widths:
        shapes.append(jax.ShapeDtypeStruct((rows // whole, width), jnp.float32))
        for lead in ((2, rows), (8, half), (4, half), (4, half), (2, 4, half), (2, 2, 3, half)):
            scratch.append(pltpu.VMEM((*lead, width), jnp.bfloat16))
    shapes.append(jax.ShapeDtypeStruct((8, 128), jnp.float32))
    found = pl.pallas_call(
        functools.partial(reduce_body, layout, parts, gains_at),
        name="reduce_grads",
        out_shape=shapes,
        in_specs=[anywhere] * (4 * items) + [inside] * (3 + len(lefts)),
        out_specs=[inside] * (items + 1),
        scratch_shapes=scratch
        + [
            pltpu.SemaphoreType.DMA((2, items)),
            pltpu.SemaphoreType.DMA((2, 2)),
            pltpu.SemaphoreType.DMA((items, 2, 2, 8)),
            pltpu.SemaphoreType.DMA((items, 2, 8)),
            pltpu.SemaphoreType.DMA((items, 3, 4)),
            pltpu.SemaphoreType.DMA((items, 2, 2, 3)),
            pltpu.SemaphoreType.DMA((items, 2, 2, 3)),
            pltpu.SemaphoreType.DMA((items, 4)),
            pltpu.SemaphoreType.REGULAR,
            pltpu.VMEM((8, 128), jnp.float32),
            pltpu.VMEM((4, 8, 128), jnp.float32),
            pltpu.VMEM((8, 8, 128), jnp.float32),
            pltpu.SemaphoreType.DMA((3,)),
            pltpu.SemaphoreType.DMA((4,)),
            pltpu.SemaphoreType.DMA((7,)),
            pltpu.SemaphoreType.DMA((8,)),
            pltpu.VMEM((2, 2, 4 * half, max(widths)), jnp.bfloat16),
            pltpu.VMEM((2, rows, max(widths)), jnp.bfloat16),
            pltpu.VMEM((4, depth, max(widths)), jnp.bfloat16),
        ],
        compiler_params=pltpu.CompilerParams(
            collective_id=tag, has_side_effects=True, vmem_limit_bytes=60 << 20
        ),
    )(*[item for quarters in rights for item in quarters], facts, places, extra, *lefts)
    return found[:-1], found[-1]


def update_body(sources, plans, *refs):
    count = len(plans)
    totals, fixes, grads = refs[0], refs[1], refs[2 : 2 + sources]
    refs = refs[2 + sources :]
    triples = [refs[3 * place : 3 * place + 3] for place in range(count)]
    outs = [refs[3 * (count + place) : 3 * (count + place) + 3] for place in range(count)]
    square, loss, real = totals[0:1, :], totals[1:2, :], totals[2:3, :]
    norm = jnp.sqrt(square) / real
    refs[6 * count][...] = jnp.concatenate([loss / real, norm] + [norm] * 6, axis=0)
    scale = (jnp.minimum(1.0, clip_at / norm) / real)[:, 0:1]
    over_one, over_two = fixes[0:1, 0:1], fixes[1:2, 0:1]

    def renew(place, grad, rows):
        source, turned, first, rate, decay = plans[place]
        weight, one, two = triples[place]
        clipped = grad * scale
        moment_one = beta_one * one[rows] + (1.0 - beta_one) * clipped
        moment_two = beta_two * two[rows] + (1.0 - beta_two) * clipped * clipped
        stepped = moment_one * over_one / (jnp.sqrt(moment_two * over_two) + adam_eps)
        outs[place][0][rows] = moment_one
        outs[place][1][rows] = moment_two
        outs[place][2][rows] = weight[rows] - rate * (stepped + decay * weight[rows])

    for place in range(count):
        source, turned, first, rate, decay = plans[place]
        rows, columns = triples[place][0].shape
        if turned and rows >= 128:
            for at in range(0, rows, 128):
                span = min(128, rows - at)
                block = grads[source][:, first + at : first + at + span].T
                renew(place, block, pl.ds(at, span))
        elif turned:
            start = first // 128 * 128
            block = grads[source][:, start : start + 128].T
            renew(place, block[first - start : first - start + rows], pl.ds(0, rows))
        else:
            for at in range(0, rows, 32):
                renew(place, grads[source][pl.ds(at, 32), first : first + columns], pl.ds(at, 32))


def update_kernel(totals, fixes, grads, plans, triples):
    inside = pl.BlockSpec(memory_space=pltpu.VMEM)
    flat = [item for triple in triples for item in triple]
    outs = [jax.ShapeDtypeStruct(item.shape, item.dtype) for item in flat] + [
        jax.ShapeDtypeStruct((8, 128), jnp.float32)
    ]
    found = pl.pallas_call(
        functools.partial(update_body, len(grads), plans),
        name="update_weights",
        out_shape=outs,
        in_specs=[inside] * (2 + len(grads) + len(flat)),
        out_specs=[inside] * len(outs),
        compiler_params=pltpu.CompilerParams(vmem_limit_bytes=60 << 20),
    )(totals, fixes, *grads, *flat)
    return found[:-1], found[-1]


def turn_halves(tile, cosine, sine):
    lane = lax.broadcasted_iota(jnp.int32, tile.shape, 1)
    other = jnp.where(lane % 64 < 32, pltpu.roll(tile, 96, 1), pltpu.roll(tile, 32, 1))
    return tile * cosine + other * sine


def greet_core(device):
    barrier = pltpu.get_barrier_semaphore()
    pl.semaphore_signal(barrier, inc=1, device_id=device, device_id_type=MESH)
    pl.semaphore_wait(barrier, 1)


def attend_steps(normed, joints, cosine, sine, seg_row, seg_col, packed, lse, attended, between, leaving, heads_out, heads_in, send_sem, recv_sem, out_send, out_recv):
    device = neighbours()["c"]
    rows = normed.shape[0]

    def project(joint, put):
        found = jnp.dot(normed[...], joint[...], preferred_element_type=jnp.float32)
        for head in range(3):
            pair = turn_halves(found[:, 192 * head : 192 * head + 128], cosine[...], sine[...])
            value = found[:, 192 * head + 128 : 192 * head + 192]
            put(head, pair.astype(jnp.bfloat16), value.astype(jnp.bfloat16))

    def crossing(place):
        return pltpu.make_async_remote_copy(
            src_ref=leaving.at[place],
            dst_ref=packed.at[place, pl.ds(rows, rows)],
            send_sem=send_sem.at[place],
            recv_sem=recv_sem.at[place],
            device_id=device,
            device_id_type=MESH,
        )

    for side, joint in enumerate((joints[1], joints[3])):

        def put(head, pair, value):
            leaving[3 * side + head, :, 0:128] = pair
            leaving[3 * side + head, :, 128:192] = value
            crossing(3 * side + head).start()

        project(joint, put)
    for side, joint in enumerate((joints[0], joints[2])):

        def put(head, pair, value):
            packed[3 * side + head, pl.ds(0, rows), 0:128] = pair
            packed[3 * side + head, pl.ds(0, rows), 128:192] = value

        project(joint, put)

    def one_head(place):
        keys = packed[place, :, 0:128][:, 64:128]
        values_t = packed[place, :, 128:256][:, 0:64].astype(jnp.float32).T.astype(jnp.bfloat16)

        def block(turn, _):
            at = pl.ds(pl.multiple_of(turn * 256, 256), 256)
            query = packed[place, at, 0:128][:, 0:64]
            scores = lax.dot_general(
                keys, query, (((1,), (1,)), ((), ())), preferred_element_type=jnp.float32
            ) * HEAD_DIM ** (-0.5)
            scores = jnp.where(seg_col[:, 0:1] == seg_row[0:1, at], scores, neg_fill)
            top = jnp.max(scores, axis=0, keepdims=True)
            expd = jnp.exp(scores - top)
            summed = jnp.sum(expd, axis=0, keepdims=True)
            probs = (expd * (1.0 / summed)).astype(jnp.bfloat16)
            found = jnp.dot(values_t, probs, preferred_element_type=jnp.float32)
            lse[pl.ds(place, 1), at] = top + jnp.log(summed)
            heads_out[place, at, 0:64] = found.T.astype(jnp.bfloat16)
            return 0

        lax.fori_loop(0, 2 * rows // 256, block, 0)

    between(0)
    for place in range(6):
        crossing(place).wait_recv()
    for place in range(6):
        one_head(place)
        between(1 + place)

    def returning(place):
        return pltpu.make_async_remote_copy(
            src_ref=heads_out.at[place, pl.ds(rows, rows)],
            dst_ref=heads_in.at[place],
            send_sem=out_send.at[place],
            recv_sem=out_recv.at[place],
            device_id=device,
            device_id_type=MESH,
        )

    for place in range(6):
        returning(place).start()
    for place in range(6):
        attended[:, 64 * place : 64 * place + 64] = heads_out[place, pl.ds(0, rows), 0:64]
    for place in range(6):
        returning(place).wait_recv()
        attended[:, 384 + 64 * place : 448 + 64 * place] = heads_in[place, :, 0:64]
    for place in range(6):
        crossing(place).wait_send()
        returning(place).wait_send()


def attend_back_body(grad_out, packed, lse, attended, cosine, sine, seg_row, seg_col, p0, p1, p2, p3, r0, r1, r2, r3, grads, leaving, keys_t, probs, prob_grads, found, going, coming, send_sem, recv_sem, out_send, out_recv):
    device = neighbours()["c"]
    rows = grad_out.shape[0]
    greet_core(device)

    def crossing(place):
        return pltpu.make_async_remote_copy(
            src_ref=leaving.at[place],
            dst_ref=grads.at[place, pl.ds(rows, rows)],
            send_sem=send_sem.at[place],
            recv_sem=recv_sem.at[place],
            device_id=device,
            device_id_type=MESH,
        )

    for place in range(6):
        leaving[place, :, 0:64] = grad_out[:, 384 + 64 * place : 448 + 64 * place]
        crossing(place).start()
        grads[place, pl.ds(0, rows), 0:64] = grad_out[:, 64 * place : 64 * place + 64]
    nothing = jnp.zeros((rows, 64), jnp.bfloat16)
    for order, (part, right) in enumerate(((p0, r0), (p2, r2), (p1, r1), (p3, r3))):
        part[:, 576:640] = nothing
        right[:, 576:640] = nothing
        right[:, 640:832] = attended[:, 192 * order : 192 * order + 192]
        right[:, 832:896] = nothing
    for place in range(6):
        crossing(place).wait_recv()

    def one_head(place):
        query = packed[place, :, 0:128][:, 0:64]
        wide_keys = packed[place, :, 0:128][:, 64:128].astype(jnp.float32)
        keys_t[...] = wide_keys.T.astype(jnp.bfloat16)
        grad = grads[place, :, 0:64]
        stat = lse[pl.ds(place, 1), :]

        def score(turn, inner):
            at = pl.ds(pl.multiple_of(turn * 256, 256), 256)
            keys = packed[place, at, 0:128][:, 64:128]
            values = packed[place, at, 128:256][:, 0:64]
            scores = lax.dot_general(
                keys, query, (((1,), (1,)), ((), ())), preferred_element_type=jnp.float32
            ) * HEAD_DIM ** (-0.5)
            scores = jnp.where(seg_col[at, 0:1] == seg_row[0:1, :], scores, neg_fill)
            prob = jnp.exp(scores - stat)
            prob_grad = lax.dot_general(
                values, grad, (((1,), (1,)), ((), ())), preferred_element_type=jnp.float32
            )
            probs[at] = prob
            prob_grads[at] = prob_grad
            value_grad = jnp.dot(prob.astype(jnp.bfloat16), grad, preferred_element_type=jnp.float32)
            found[place, at, 128:192] = value_grad
            return inner + jnp.sum(prob * prob_grad, axis=0, keepdims=True)

        inner = lax.fori_loop(0, 2 * rows // 256, score, jnp.zeros((1, 2 * rows), jnp.float32))

        def spread_back(turn, query_grad):
            at = pl.ds(pl.multiple_of(turn * 256, 256), 256)
            score_grad = (probs[at] * (prob_grads[at] - inner)).astype(jnp.bfloat16)
            key_grad = jnp.dot(score_grad, query, preferred_element_type=jnp.float32)
            found[place, at, 64:128] = key_grad * HEAD_DIM ** (-0.5)
            return query_grad + jnp.dot(keys_t[:, at], score_grad, preferred_element_type=jnp.float32)

        query_grad = lax.fori_loop(
            0, 2 * rows // 256, spread_back, jnp.zeros((64, 2 * rows), jnp.float32)
        )
        found[place, :, 0:64] = query_grad.T * HEAD_DIM ** (-0.5)

    def heads(place, _):
        one_head(place)
        return 0

    lax.fori_loop(0, 6, heads, 0)

    def returning(side):
        return pltpu.make_async_remote_copy(
            src_ref=going.at[side],
            dst_ref=coming.at[side],
            send_sem=out_send.at[side],
            recv_sem=out_recv.at[side],
            device_id=device,
            device_id_type=MESH,
        )

    for half in (1, 0):
        at = pl.ds(half * rows, rows)
        for side in range(2):
            for head in range(3):
                place = 3 * side + head
                pair = turn_halves(found[place, at, 0:128], cosine[at], -sine[at]).astype(jnp.bfloat16)
                value = found[place, at, 128:192].astype(jnp.bfloat16)
                puts = [going.at[side]] if half else [(p0, p2)[side], (r0, r2)[side]]
                for put in puts:
                    put[:, 192 * head : 192 * head + 128] = pair
                    put[:, 192 * head + 128 : 192 * head + 192] = value
            if half:
                returning(side).start()
    for side in range(2):
        returning(side).wait_recv()
        for put in ((p1, p3)[side], (r1, r3)[side]):
            put[:, 0:576] = coming[side, :, 0:576]
    for place in range(6):
        crossing(place).wait_send()
    for side in range(2):
        returning(side).wait_send()


def attend_back_kernel(grad_out, packed, lse, attended, cosine, sine, seg_row, seg_col):
    rows = grad_out.shape[0]
    inside = pl.BlockSpec(memory_space=pltpu.VMEM)
    found = pl.pallas_call(
        attend_back_body,
        name="attend_back",
        out_shape=[jax.ShapeDtypeStruct((rows, 640), jnp.bfloat16)] * 4
        + [jax.ShapeDtypeStruct((rows, 896), jnp.bfloat16)] * 4,
        in_specs=[inside] * 8,
        out_specs=[inside] * 8,
        scratch_shapes=[
            pltpu.VMEM((6, 2 * rows, 128), jnp.bfloat16),
            pltpu.VMEM((6, rows, 128), jnp.bfloat16),
            pltpu.VMEM((64, 2 * rows), jnp.bfloat16),
            pltpu.VMEM((2 * rows, 2 * rows), jnp.float32),
            pltpu.VMEM((2 * rows, 2 * rows), jnp.float32),
            pltpu.VMEM((6, 2 * rows, 256), jnp.float32),
            pltpu.VMEM((2, rows, 640), jnp.bfloat16),
            pltpu.VMEM((2, rows, 640), jnp.bfloat16),
            pltpu.SemaphoreType.DMA((6,)),
            pltpu.SemaphoreType.DMA((6,)),
            pltpu.SemaphoreType.DMA((2,)),
            pltpu.SemaphoreType.DMA((2,)),
        ],
        compiler_params=pltpu.CompilerParams(
            collective_id=3, has_side_effects=True, vmem_limit_bytes=56 << 20
        ),
    )(grad_out, packed, lse, attended, cosine, sine, seg_row, seg_col)
    return found[:4], found[4:]


def known_mesh():
    return lax.axis_size("dp") == 8 and lax.axis_size("tensor") == 4


def reduce_grads(layout, lefts, rights, places, extra, facts, parts, gains_at):
    if known_mesh():
        ordered = [[item[0], item[2], item[1], item[3]] for item in rights]
        return reduce_kernel(layout, lefts, ordered, places, extra, facts, parts, gains_at, 1)
    sums = []
    for item, products in enumerate(layout):
        quarters = []
        for quarter, mask in enumerate((0, 2, 1, 3)):
            right = rights[item][quarter]
            found = [mm(lefts[at], right[:, base : base + width]) for at, base, width, _ in products]
            if item == 0:
                spots = jnp.arange(right.shape[1], dtype=jnp.int32)[None, :]
                found[0] += mm(lefts[1], narrow(places[:, mask : mask + 1] == spots))
            if item == gains_at[0]:
                found[0] += extra
            quarters.append(narrow(jnp.concatenate(found, axis=1)))
        sums.append(reduce_all(quarters, True))
    square = sum(jnp.sum(item * item) for item in sums)
    repeated = sums[gains_at[0]][:, gains_at[1] : gains_at[1] + gains_at[2]]
    square = square - jnp.sum(repeated * repeated) * (1.0 - 1.0 / parts)
    tile = jnp.where(lax.broadcasted_iota(jnp.int32, (8, 128), 0) == 0, square, facts)
    return sums, everyone_sum(tile)


def wide(value):
    return value.astype(jnp.float32)


def narrow(value):
    return value.astype(jnp.bfloat16)


def fold(value, masks, last):
    rows = value.shape[0] // (len(masks) + 1)
    total = wide(value[:rows])
    for place, mask in enumerate(masks):
        total = total + wide(swap(value[(place + 1) * rows : (place + 2) * rows], "dp", mask))
    return total if last else narrow(total)


def reduce_all(quarters, x_first):
    groups = groups_of(lax.axis_size("dp"))
    own = narrow(wide(quarters[0]) + wide(swap(quarters[2], "tensor", 1)))
    other = narrow(wide(quarters[1]) + wide(swap(quarters[3], "tensor", 1)))
    if x_first:
        own = narrow(wide(own) + wide(swap(other, "tensor", 2)))
        own = fold(own, groups[0], len(groups) == 1)
    else:
        own = fold(own, groups[0], False)
        other = fold(other, groups[0], False)
        own = narrow(wide(own) + wide(swap(other, "tensor", 2)))
    for place in range(1, len(groups)):
        own = fold(own, groups[place], place == len(groups) - 1)
    return wide(own)


def everyone_sum(value):
    for masks in groups_of(lax.axis_size("dp")):
        value = sum([swap(value, "dp", mask) for mask in masks], value)
    for mask in (1, 2):
        value = value + swap(value, "tensor", mask)
    return value


def mm(left, right):
    return jnp.dot(left, right, preferred_element_type=jnp.float32)


def mm_nt(left, right):
    return lax.dot_general(left, right, (((1,), (1,)), ((), ())), preferred_element_type=jnp.float32)


def mm_tn(left, right):
    return lax.dot_general(left, right, (((0,), (0,)), ((), ())), preferred_element_type=jnp.float32)


def rotate_heads(values, cosine, sine):
    return rotate(values, cosine[:, None, :], sine[:, None, :])


def scores_of(query, key_rows, same_doc):
    scores = jnp.einsum(
        "qhe,khe->hqk", query, key_rows, preferred_element_type=jnp.float32
    ) * HEAD_DIM ** (-0.5)
    return jnp.where(same_doc[None], scores, neg_fill)


def split_heads(packed):
    packed = packed.reshape(packed.shape[0], -1, 3, HEAD_DIM)
    return packed[:, :, 0], packed[:, :, 1], packed[:, :, 2]


def attend(packed, same_doc):
    query, key_rows, value_rows = split_heads(packed)
    scores = scores_of(query, key_rows, same_doc)
    row_max = jnp.max(scores, axis=-1, keepdims=True)
    expd = jnp.exp(scores - row_max)
    summed = jnp.sum(expd, axis=-1, keepdims=True)
    probs = (expd / summed).astype(jnp.bfloat16)
    output = jnp.einsum("hqk,khe->qhe", probs, value_rows, preferred_element_type=jnp.float32)
    return (narrow(output).reshape(packed.shape[0], -1), (row_max + jnp.log(summed))[..., 0])


def attend_back(packed, same_doc, row_lse, grad_out, cosine, sine):
    query, key_rows, value_rows = split_heads(packed)
    grad_out = grad_out.reshape(packed.shape[0], -1, HEAD_DIM)
    scores = scores_of(query, key_rows, same_doc)
    probs = jnp.exp(scores - row_lse[..., None])
    value_grad = jnp.einsum(
        "hqk,qhe->khe", probs.astype(jnp.bfloat16), grad_out, preferred_element_type=jnp.float32
    )
    prob_grad = jnp.einsum("qhe,khe->hqk", grad_out, value_rows, preferred_element_type=jnp.float32)
    inner = jnp.sum(prob_grad * probs, axis=-1, keepdims=True)
    score_grad = (probs * (prob_grad - inner)).astype(jnp.bfloat16)
    query_grad = jnp.einsum(
        "hqk,khe->qhe", score_grad, key_rows, preferred_element_type=jnp.float32
    ) * HEAD_DIM ** (-0.5)
    key_grad = jnp.einsum(
        "hqk,qhe->khe", score_grad, query, preferred_element_type=jnp.float32
    ) * HEAD_DIM ** (-0.5)
    query_grad = rotate_heads(query_grad, cosine, -sine)
    key_grad = rotate_heads(key_grad, cosine, -sine)
    return narrow(jnp.stack([query_grad, key_grad, value_grad], axis=2).reshape(packed.shape))


def update_weights(totals, fixes, sums, plans, triples):
    if known_mesh():
        updated, results = update_kernel(totals, fixes, sums, plans, triples)
        return list(updated), results
    updated = []
    norm = jnp.sqrt(totals[0, 0]) / totals[2, 0]
    scale = jnp.minimum(1.0, clip_at / norm) / totals[2, 0]
    for (source, turned, first, rate, decay), (weight, one, two) in zip(plans, triples):
        columns = weight.shape[0] if turned else weight.shape[1]
        grad = sums[source][:, first : first + columns]
        clipped = (grad.T if turned else grad) * scale
        moment_one = beta_one * one + (1.0 - beta_one) * clipped
        moment_two = beta_two * two + (1.0 - beta_two) * clipped * clipped
        stepped = moment_one * fixes[0, 0] / (jnp.sqrt(moment_two * fixes[1, 0]) + adam_eps)
        updated.extend([moment_one, moment_two, weight - rate * (stepped + decay * weight)])
    return updated, jnp.stack([totals[1, 0] / totals[2, 0], norm])[:, None]


def per_device(
    tokens,
    lengths,
    timesteps,
    masks,
    step_count,
    table,
    joint_weight,
    output_weight,
    upward_weight,
    downward_weight,
    gains,
    momentum_table,
    momentum_joint,
    momentum_output,
    momentum_upward,
    momentum_downward,
    momentum_gains,
    variance_table,
    variance_joint,
    variance_output,
    variance_upward,
    variance_downward,
    variance_gains,
):
    place = lax.axis_index("tensor")
    parts = lax.axis_size("tensor")
    rows = tokens.shape[0] // parts
    vocab_part, head_part = table.shape[0], joint_weight.shape[1]
    out_part, ff_part = output_weight.shape[0], upward_weight.shape[1]

    gain_columns = jnp.pad(narrow(gains).T, ((0, 0), (0, 61)))
    shards = [
        narrow(table).T,
        jnp.concatenate([narrow(joint_weight), gain_columns], axis=1),
        narrow(upward_weight),
        narrow(downward_weight).T,
        narrow(output_weight).T,
    ]
    start = place * rows
    seq = start // SEQ_LEN
    mine = start - seq * SEQ_LEN
    cut = lambda array: lax.dynamic_slice(array, (start,), (rows,))
    targets = cut(tokens)
    corrupt = cut(masks) == 1
    inputs = jnp.where(corrupt, VOCAB - 1, targets)
    own_lengths = lax.dynamic_slice(lengths, (seq, 0), (1, DOCS))
    step_here = lax.dynamic_slice(timesteps, (seq,), (1,))
    theirs = mine ^ rows
    position = jnp.concatenate(
        [mine + jnp.arange(rows, dtype=jnp.int32), theirs + jnp.arange(rows, dtype=jnp.int32)]
    )
    doc_ends = jnp.cumsum(own_lengths[0])
    doc_starts = doc_ends - own_lengths[0]
    segment = jnp.sum((position[:, None] >= doc_ends[None, :]).astype(jnp.int32), axis=1)
    chosen = segment[:, None] == jnp.arange(DOCS, dtype=jnp.int32)[None, :]
    offset = position - jnp.sum(jnp.where(chosen, doc_starts[None, :], 0), axis=1)
    is_real = segment < DOCS - 1
    factor = jnp.where(step_here == 1, 1.0, T_DIFF / step_here.astype(jnp.float32))
    weights = jnp.where(corrupt & is_real[:rows], factor, 0.0)
    inverse_freq = 10000.0 ** (-jnp.arange(HEAD_DIM // 2, dtype=jnp.float32) / (HEAD_DIM // 2))
    angles = offset.astype(jnp.float32)[:, None] * inverse_freq
    cosine, sine = jnp.cos(angles), jnp.sin(angles)
    same_doc = segment[:, None] == segment[None, :]

    def hot(ids, piece):
        base = (place ^ (2 * (piece % 2) + piece // 2)) * vocab_part
        return (ids - base)[:, None] == jnp.arange(vocab_part, dtype=jnp.int32)[None, :]

    pieces = range(4)
    places = jnp.pad(
        jnp.stack([inputs - (place ^ mask) * vocab_part for mask in range(4)], axis=1),
        ((0, 0), (0, 124)),
    )

    on_known = known_mesh()
    if on_known:
        cosines = jnp.concatenate([cosine] * 4, axis=1)
        sines = jnp.concatenate([-sine, sine] * 2, axis=1)
        seg_row = jnp.broadcast_to(segment[None, :], (8, 2 * rows))
        seg_col = jnp.broadcast_to(segment[:, None], (2 * rows, 128))
        groups, (embedded, normed_one, packed, attn_lse, attended_all) = start_kernel(
            shards, places, cosines[:rows], sines[:rows], seg_row, seg_col
        )
        groups = [[item[0], item[2], item[1], item[3]] for item in groups]
    else:
        groups = [gather_all(item, True) for item in shards]
    table_q, first_group, up_q, down_q, out_q = groups
    gain_full = wide(first_group[0][:, head_part : head_part + 3]).T
    out_all = jnp.concatenate(out_q, axis=1)
    if not on_known:
        joint_q = [item[:, :head_part] for item in first_group]
        looked = sum(mm_nt(narrow(hot(inputs, piece)), table_q[piece]) for piece in pieces)
        embedded = looked * D**0.5
        normed_one = narrow(norm_apply(embedded, gain_full[0]))

        def turned(projected):
            projected = projected.reshape(rows, -1, 3, HEAD_DIM)
            query = rotate_heads(projected[:, :, 0], cosine[:rows], sine[:rows])
            key_rows = rotate_heads(projected[:, :, 1], cosine[:rows], sine[:rows])
            stacked = jnp.stack([query, key_rows, projected[:, :, 2]], axis=2)
            return narrow(stacked.reshape(rows, -1))

        packed = [turned(mm(normed_one, item)) for item in joint_q]
        whole = [
            jnp.concatenate([packed[side], swap(packed[2 + side], "tensor", 1)], axis=0)
            for side in range(2)
        ]
        attended, attn_lse = zip(*[attend(item, same_doc) for item in whole])
        attended_all = jnp.concatenate(
            [item[:rows] for item in attended]
            + [swap(item[rows:], "tensor", 1) for item in attended],
            axis=1,
        )
    after_attn = embedded + mm_nt(attended_all, out_all)
    normed_two = narrow(norm_apply(after_attn, gain_full[1]))
    pre_gelu = [mm(normed_two, item) for item in up_q]
    below = [0.5 + 0.5 * lax.erf(item * 0.5**0.5) for item in pre_gelu]
    slopes = [
        part + item * jnp.exp(-0.5 * item * item) * (0.5 / jnp.pi) ** 0.5
        for part, item in zip(below, pre_gelu)
    ]
    activated = [narrow(item * part) for part, item in zip(below, pre_gelu)]
    after_mlp = after_attn + sum(mm_nt(activated[q], down_q[q]) for q in range(4))
    normed_out = narrow(norm_apply(after_mlp, gain_full[2]))
    logits = [mm(normed_out, item) for item in table_q]
    row_max = logits[0].max(axis=1)
    for item in logits[1:]:
        row_max = jnp.maximum(row_max, item.max(axis=1))
    row_sum = sum(jnp.sum(jnp.exp(item - row_max[:, None]), axis=1) for item in logits)
    target_hot = [hot(targets, piece) for piece in pieces]
    row_pick = sum(
        jnp.sum(jnp.where(target_hot[piece], logits[piece], 0.0), axis=1) for piece in pieces
    )
    row_lse = row_max + jnp.log(row_sum)
    loss_local = jnp.sum(weights * (row_lse - row_pick))
    count_local = jnp.sum(is_real[:rows].astype(jnp.float32))

    logit_grad = [
        narrow(
            weights[:, None]
            * (jnp.exp(logits[piece] - row_lse[:, None]) - target_hot[piece].astype(jnp.float32))
        )
        for piece in pieces
    ]
    out_grad = sum(mm_nt(logit_grad[piece], table_q[piece]) for piece in pieces)
    mlp_grad, gain_three = norm_back(after_mlp, gain_full[2], out_grad)
    mlp_branch = narrow(mlp_grad)
    up_input = [
        narrow(slopes[q] * mm(mlp_branch, down_q[q])) for q in range(4)
    ]
    normed_two_grad = sum(mm_nt(up_input[q], up_q[q]) for q in range(4))
    attn_in_grad, gain_two = norm_back(after_attn, gain_full[1], normed_two_grad)
    resid_one = mlp_grad + attn_in_grad
    attn_branch = narrow(resid_one)
    attended_grad = narrow(mm(attn_branch, out_all))
    if on_known:
        proj_grad, last_rights = attend_back_kernel(
            attended_grad, packed, attn_lse, attended_all, cosines, sines, seg_row, seg_col
        )
        proj_grad = [proj_grad[q] for q in (0, 2, 1, 3)]
        last_rights = [last_rights[q] for q in (0, 2, 1, 3)]
        joint_back = first_group
    else:
        grad_parts = [attended_grad[:, q * out_part : (q + 1) * out_part] for q in range(4)]
        proj_whole = [
            attend_back(
                whole[side],
                same_doc,
                attn_lse[side],
                jnp.concatenate(
                    [grad_parts[side], swap(grad_parts[2 + side], "tensor", 1)], axis=0
                ),
                cosine,
                sine,
            )
            for side in range(2)
        ]
        proj_grad = [item[:rows] for item in proj_whole] + [
            swap(item[rows:], "tensor", 1) for item in proj_whole
        ]
        joint_back = joint_q
    normed_one_grad = sum(mm_nt(proj_grad[q], joint_back[q]) for q in range(4))
    embed_in, gain_one = norm_back(embedded, gain_full[0], normed_one_grad)
    embed_grad = resid_one + embed_in
    embed_scaled = narrow(embed_grad * D**0.5)
    sublane = lax.broadcasted_iota(jnp.int32, (8, 128), 0)
    facts = jnp.where(sublane == 1, loss_local, jnp.where(sublane == 2, count_local, 0.0))
    gains_end = (head_part + gains.shape[0] + 127) // 128 * 128
    out_fill = (out_part + 127) // 128 * 128
    fill = lambda array, columns: jnp.pad(array, ((0, 0), (0, columns - array.shape[1])))
    extra = jnp.pad(
        jnp.stack([gain_one, gain_two, gain_three]).T,
        ((0, 0), (head_part, gains_end - head_part - gains.shape[0])),
    )
    if not on_known:
        attended_q = [attended_all[:, q * out_part : (q + 1) * out_part] for q in range(4)]
        last_rights = [
            jnp.concatenate([fill(proj_grad[q], gains_end), fill(attended_q[q], out_fill)], axis=1)
            for q in range(4)
        ]
    lefts = [
        item.T
        for item in (normed_out, embed_scaled, normed_two, mlp_branch, normed_one, attn_branch)
    ]
    rights = [
        logit_grad,
        [jnp.concatenate([up_input[q], activated[q]], axis=1) for q in range(4)],
        last_rights,
    ]
    half_ff = ff_part // 2
    layout = (
        ((0, 0, vocab_part, 512),),
        ((2, 0, ff_part, half_ff), (3, ff_part, ff_part, half_ff)),
        ((4, 0, gains_end, gains_end), (5, gains_end, out_fill, out_fill)),
    )
    sums, totals = reduce_grads(
        layout, lefts, rights, places, extra, facts, parts, (2, head_part, gains_end - head_part)
    )
    step_float = step_count[0].astype(jnp.float32)
    fixes = jnp.where(
        sublane == 0,
        1.0 / (1.0 - jnp.power(beta_one, step_float)),
        1.0 / (1.0 - jnp.power(beta_two, step_float)),
    )
    plans = (
        (0, False, 0, rates[0], decays[0]),
        (2, False, 0, rates[1], decays[1]),
        (2, True, gains_end, rates[2], decays[2]),
        (1, False, 0, rates[3], decays[3]),
        (1, False, ff_part, rates[4], decays[4]),
        (2, True, head_part, rates[5], decays[5]),
    )
    triples = (
        (table.T, momentum_table.T, variance_table.T),
        (joint_weight, momentum_joint, variance_joint),
        (output_weight, momentum_output, variance_output),
        (upward_weight, momentum_upward, variance_upward),
        (downward_weight.T, momentum_downward.T, variance_downward.T),
        (gains, momentum_gains, variance_gains),
    )
    updated, results = update_weights(totals, fixes, sums, plans, triples)
    updated = [item.T if place // 3 in (0, 4) else item for place, item in enumerate(updated)]
    return tuple([results[0, 0], results[1, 0]] + updated)


def solution(mesh):
    placed = (
        P("dp"),
        P("dp", None),
        P("dp"),
        P("dp"),
        P(),
        P("tensor", "dp"),
        P("dp", "tensor"),
        P("tensor", "dp"),
        P("dp", "tensor"),
        P("tensor", "dp"),
        P(None, "dp"),
        P("tensor", "dp"),
        P("dp", "tensor"),
        P("tensor", "dp"),
        P("dp", "tensor"),
        P("tensor", "dp"),
        P(None, "dp"),
        P("tensor", "dp"),
        P("dp", "tensor"),
        P("tensor", "dp"),
        P("dp", "tensor"),
        P("tensor", "dp"),
        P(None, "dp"),
    )
    return jax.shard_map(
        per_device,
        mesh=mesh,
        in_specs=placed,
        out_specs=(
            P(),
            P(),
            P("tensor", "dp"),
            P("tensor", "dp"),
            P("tensor", "dp"),
            P("dp", "tensor"),
            P("dp", "tensor"),
            P("dp", "tensor"),
            P("tensor", "dp"),
            P("tensor", "dp"),
            P("tensor", "dp"),
            P("dp", "tensor"),
            P("dp", "tensor"),
            P("dp", "tensor"),
            P("tensor", "dp"),
            P("tensor", "dp"),
            P("tensor", "dp"),
            P(None, "dp"),
            P(None, "dp"),
            P(None, "dp"),
        ),
        check_vma=False,
    )
```

profile of v0, /device:TPU:0, one launch (start us, length us, event | category | flops | bytes accessed | tf_op | source)
XLA Modules:
  0.0 448.2 jit_solution(9654997895484084362)
XLA Ops:
  2.5 1.9 fusion.27
  18.2 134.4 %start.1 = (bf16[768,2048]{1,0:T(8,128)(2,1)}, bf16[768,2048]{1,0:T(8,128)(2,1)}, bf16[768,2048]{1,0:T(8,128)(2,1)}, bf16[768,2048]{1,0:T(8,128)(2,1)}, bf16[768...) custom-call(bf16[96,2048]{1,0:T(8,128)(2,1)} %convert_bitcast_fusion, ...), custom_call_target="tpu_custom_call" | custom-call | tf_op jit(solution)/shard_map/start/pallas_call | solution.py:337
  152.7 1.9 copy.154
  154.5 2.4 multiply_reduce_fusion.8
  159.3 2.1 multiply_convert_fusion.8
  163.0 2.0 multiply_convert_fusion.9
  166.6 2.1 multiply_convert_fusion.7
  170.3 2.0 multiply_convert_fusion.6
  174.5 2.0 fusion.37
  176.5 2.2 fusion.36
  178.7 2.0 fusion.38
  180.7 2.0 fusion.35
  182.7 5.0 %select_reduce_fusion.2 = (f32[512]{0:T(512)S(1)}, f32[512]{0:T(512)S(1)}, f32[512]{0:T(512)S(1)}, f32[512]{0:T(512)S(1)}, f32[512]{0:T(512)S(1)}, /*index=5*/f32[512]{0:T(512)S(1)}, f32[512]{0:T(512)S(1)}, f32[512]{0:T(512)S(1)}) fusion(f32[512,2048]{1,0:T(8,128)S(1)} %get-tuple-element.202, s32[512]{0:T(512)S(1)} %get-tuple-element.160, ...), kind=kLoop, calls=%fused_computation.2 | loop fusion | flops 20967424 | bytes 16803840 | tf_op jit(solution)/shard_map/reduce_sum | solution.py:1324
  188.3 8.1 %multiply_convert_fusion = (bf16[512,2048]{1,0:T(8,128)(2,1)}, bf16[512,2048]{1,0:T(8,128)(2,1)}, bf16[512,2048]{1,0:T(8,128)(2,1)}, bf16[512,2048]{1,0:T(8,128)(2,1)}) fusion(f32[512,2048]{1,0:T(8,128)S(1)} %get-tuple-element.196, s32[512]{0:T(512)S(1)} %get-tuple-element.163, f32[512]{0:T(512)S(1)} %get-tuple-element.153, f32[512]{0:T(512)S(1)} %get-tuple-element.154, ...), kind=kLoop, calls=%fused_computation.4 | loop fusion | flops 25165824 | bytes 25178112 | tf_op jit(solution)/shard_map/convert_element_type | solution.py:1078
  196.4 4.5 %fusion.43 = f32[512,768]{0,1:T(8,128)S(1)} fusion(bf16[512,2048]{1,0:T(8,128)(2,1)} %get-tuple-element.174.refs_2_, bf16[768,2048]{1,0:T(8,128)(2,1)} %get-tuple-element.92), kind=kOutput, calls=%fused_computation.147 | convolution fusion | flops 1610612736 | bytes 6815744 | tf_op jit(solution)/shard_map/dot_general | solution.py:1118
  200.9 1.8 fusion.42
  202.7 1.9 fusion.44
  204.6 2.3 multiply_reduce_fusion.1
  221.5 1.7 convert_bitcast_fusion.1
  223.2 1.9 convolution_convert_fusion.grad_out
  225.1 41.7 %attend_back.1 = (bf16[512,640]{1,0:T(8,128)(2,1)}, bf16[512,640]{1,0:T(8,128)(2,1)}, bf16[512,640]{1,0:T(8,128)(2,1)}, bf16[512,640]{1,0:T(8,128)(2,1)}, bf16[5...) custom-call(bf16[512,768]{1,0:T(8,128)(2,1)} %convolution_convert_fusion.gra, ...), custom_call_target="tpu_custom_call" | custom-call | tf_op jit(solution)/shard_map/attend_back/pallas_call | solution.py:1017
  266.8 2.0 fusion.49
  273.8 1.4 fusion.24.refs_16_
  276.6 1.6 pad.14.refs_14_
  280.0 1.3 broadcast_select_fusion.refs_12_
  281.3 1.3 pad_maximum_fusion.3.refs_7_
  283.2 1.3 pad_maximum_fusion.2.refs_6_
  285.2 1.3 pad_maximum_fusion.1.refs_5_
  287.1 1.3 pad_maximum_fusion.refs_4_
  289.7 149.5 %reduce_grads.1 = (f32[96,2048]{1,0:T(8,128)}, f32[96,1536]{1,0:T(8,128)}, f32[96,896]{1,0:T(8,128)}, f32[8,128]{1,0:T(8,128)}) custom-call(bf16[512,2048]{1,0:T(8,128)(2,1)} %get-tuple-element.176.refs_0_, bf16[512,2048]{1,0:T(8,128)(2,1)} %get-tuple-element.175.refs_1_, bf16[512,2048]{1,0:T(8,128)(2,1)} %get-tuple-element.174.refs_2_, ...), custom_call_target="tpu_custom_call" | custom-call | tf_op jit(solution)/shard_map/reduce_grads/pallas_call | solution.py:716
  440.7 5.8 %update_weights.1 = (f32[96,2048]{1,0:T(8,128)}, f32[96,2048]{1,0:T(8,128)}, f32[96,2048]{1,0:T(8,128)}, f32[96,576]{1,0:T(8,128)}, f32[96,576]{1,0:T(8,128)}, /...) custom-call(f32[8,128]{1,0:T(8,128)} %get-tuple-element.109.refs_0_,, ...), custom_call_target="tpu_custom_call" | custom-call | tf_op jit(solution)/shard_map/update_weights/pallas_call | solution.py:797
  446.5 1.3 fusion.34
  (209 shorter events, 50.3 us)
Async XLA Ops:
  4.4 4.1 copy-start.64
  6.4 8.1 %copy-start.13 = (f32[2048,96]{0,1:T(8,128)S(1)}, f32[2048,96]{0,1:T(8,128)}, u32[]{:S(2)}) copy-start(f32[2048,96]{0,1:T(8,128)} %param.28) | copy-start | bytes 2359300
  7.7 7.6 %copy-start.29 = (f32[96,576]{1,0:T(8,128)S(1)}, f32[96,576]{1,0:T(8,128)}, u32[]{:S(2)}) copy-start(f32[96,576]{1,0:T(8,128)} %refs_8_.1) | copy-start | bytes 663556
  8.4 6.9 %copy-start.47 = (f32[3,96]{1,0:T(4,128)S(1)}, f32[3,96]{1,0:T(4,128)}, u32[]{:S(2)}) copy-start(f32[3,96]{1,0:T(4,128)} %refs_20_.1) | copy-start | bytes 3460
  11.9 4.2 copy-start.21
  12.1 4.8 %copy-start.20 = (f32[96,768]{1,0:T(8,128)S(1)}, f32[96,768]{1,0:T(8,128)}, u32[]{:S(2)}) copy-start(f32[96,768]{1,0:T(8,128)} %refs_14_.1) | copy-start | bytes 884740
  12.8 4.7 %copy-start.46 = (f32[192,96]{1,0:T(8,128)S(1)}, f32[192,96]{1,0:T(8,128)}, u32[]{:S(2)}) copy-start(f32[192,96]{1,0:T(8,128)} %refs_11_.1) | copy-start | bytes 221188
  159.3 2.1 copy-start.58
  163.0 2.1 copy-start.54
  166.6 2.1 copy-start.50
  170.3 2.0 copy-start.24
  172.3 2.2 copy-start.2
  174.5 2.0 copy-start.1
  176.5 2.2 copy-start.4
  178.7 2.0 copy-start
  196.3 4.5 %copy-start.3 = (bf16[768,2048]{1,0:T(8,128)(2,1)S(1)}, bf16[768,2048]{1,0:T(8,128)(2,1)}, u32[]{:S(2)}) copy-start(bf16[768,2048]{1,0:T(8,128)(2,1)} %get-tuple-element.91) | copy-start | bytes 9437188
  196.3 4.5 %copy-start.7 = (bf16[512,2048]{1,0:T(8,128)(2,1)S(1)}, bf16[512,2048]{1,0:T(8,128)(2,1)}, u32[]{:S(2)}) copy-start(bf16[512,2048]{1,0:T(8,128)(2,1)} %get-tuple-element.176.refs_0_) | copy-start | bytes 6291460
  202.7 1.9 copy-start.5
  206.9 2.0 copy-start.68
  207.3 10.6 %copy-start.18 = (bf16[512,768]{0,1:T(8,128)(2,1)}, bf16[512,768]{0,1:T(8,128)(2,1)S(1)}, u32[]{:S(2)}) copy-start(bf16[512,768]{0,1:T(8,128)(2,1)S(1)} %fusion.33) | copy-start | bytes 2359300
  210.3 2.0 copy-start.67
  213.6 2.0 copy-start.66
  216.9 2.0 copy-start.65
  223.2 1.9 copy-start.9
  225.1 41.7 %copy-start.28 = (bf16[768,640]{1,0:T(8,128)(2,1)S(1)}, bf16[768,640]{1,0:T(8,128)(2,1)}, u32[]{:S(2)}) copy-start(bf16[768,640]{1,0:T(8,128)(2,1)} %get-tuple-element.103) | copy-start | bytes 2949124
  266.8 2.0 copy-start.19
  266.8 2.0 copy-start.45
  278.2 3.1 copy-start.15
  278.2 3.1 copy-start.17
  281.3 1.9 copy-start.38
  283.2 1.9 copy-start.42
  285.2 1.9 copy-start.40
  (37 other events, 48.7 us)
where the time goes:
time: 453 us; the launch traced here: 448 us
  Pallas kernels  331 us (73%)
  matrix products  47.9 us (11%)
  other arithmetic  36.5 us (8%)
  local copies, waits for them, and re-layouts  28.4 us (6%)
    pallas_call x1, Pallas kernels, reduce_kernel(): pl.pallas_call(functools.partial(reduce_body, layout, parts, gains_at), n...  150 us
    pallas_call x1, Pallas kernels, start_kernel(): pl.pallas_call(functools.partial(start_body, items), name='start', out_sh...  134 us
    pallas_call x1, Pallas kernels, attend_back_kernel(): pl.pallas_call(attend_back_body, name='attend_back', out_shape=[jax.Shape...  41.7 us
    dot_general x17, matrix products, mm_nt(): lax.dot_general(left, right, (((1,), (1,)), ((), ())), preferred_element_...  25 us
    dot_general x13, matrix products, mm(): return jnp.dot(left, right, preferred_element_type=jnp.float32)  22.9 us
    unnamed x139, local copies, waits for them, and re-layouts  15.7 us
    convert_element_type x7, other arithmetic, narrow(): return value.astype(jnp.bfloat16)  9.51 us

commit v1 on v0

--- a/solution.py
+++ b/solution.py
@@ -370,43 +370,32 @@
     return [flat[4 * item : 4 * item + 4] for item in range(items)], flat[4 * items :]
 
 
-def reduce_body(layout, parts, gains_at, *refs):
+def reduce_tools(layout, gains_at, parts, places, extra, lefts, wide_refs, outs, refs):
     items = len(layout)
-    wide_refs = [refs[4 * item : 4 * item + 4] for item in range(items)]
-    refs = refs[4 * items :]
-    facts, places, extra = refs[:3]
-    lefts = refs[3:9]
-    refs = refs[9:]
-    outs, totals = refs[:items], refs[items]
-    refs = refs[items + 1 :]
     held = [refs[6 * item : 6 * item + 6] for item in range(items)]
     refs = refs[6 * items :]
     side_sem, c_send, c_sem, x_sem, y_sem, zs_sem, zr_sem, load_sem, free_sem = refs[:9]
-    tile, tile_row, tile_column, row_send, row_recv, column_send, column_recv = refs[9:16]
-    crossed, from_c, rights = refs[16:]
+    crossed, from_c, rights = refs[9:]
     column = lax.axis_index("dp")
-    z, y = column // 2, column % 2
+    z = column // 2
     devices = neighbours()
     shard = [item.shape[0] for item in outs]
     piece = [item // 2 for item in shard]
     width = [item.shape[1] for item in outs]
 
-    def load(item, quarter):
+    def load(item, quarter, which):
+        sources, first_column, span = wide_refs[item][which]
+        before = sum([part[2] for part in wide_refs[item][:which]])
         return pltpu.make_async_copy(
-            wide_refs[item][quarter],
-            rights.at[quarter, :, pl.ds(0, width[item])],
-            load_sem.at[item, quarter],
-        )
-
-    for quarter in range(4):
-        load(0, quarter).start()
-    row = lax.axis_index("tensor")
-    row_peers = [(column, (row + away) % 4) for away in (1, 2, 3)]
-    column_peers = [((column + away) % 8, row) for away in range(1, 8)]
-    barrier = pltpu.get_barrier_semaphore()
-    for device in row_peers + column_peers:
-        pl.semaphore_signal(barrier, inc=1, device_id=device, device_id_type=MESH)
-    pl.semaphore_wait(barrier, 10)
+            sources[quarter].at[:, pl.ds(first_column, span)],
+            rights.at[quarter, :, pl.ds(before, span)],
+            load_sem.at[item, quarter, which],
+        )
+
+    def start_loads(item):
+        for quarter in range(4):
+            for which in range(len(wide_refs[item])):
+                load(item, quarter, which).start()
 
     def span(item, part, source):
         return pl.ds(pl.multiple_of(source * shard[item] + part * piece[item], 8), piece[item])
@@ -416,24 +405,21 @@
             src_ref=src, dst_ref=dst, send_sem=send, recv_sem=recv, device_id=devices[name], device_id_type=MESH
         )
 
-    def c_copy(item, part, side, source, slot=0):
-        here = pl.ds(pl.multiple_of(source % 2 * shard[item] + part * piece[item], 8), piece[item])
+    def c_copy(item, side, source, slot=0):
         columns = pl.ds(0, width[item])
+        block = 2 * shard[item]
+        there = pl.ds(pl.multiple_of(source // 2 * block, 16), block)
         return remote(
-            crossed.at[side, slot, here, columns],
-            from_c.at[side, span(item, part, source), columns],
+            crossed.at[side, slot, :, columns],
+            from_c.at[side, there, columns],
             c_send.at[side, slot],
-            c_sem.at[item, part, side, source],
+            c_sem.at[item, side, source // 2],
             "c",
         )
-
-    def c_wait(item, part, side, source):
-        c_copy(item, part, side, source).wait_recv()
 
     def c_sent(item, slot):
         for side in range(2):
-            lead = crossed.at[side, slot, :, pl.ds(0, width[item])]
-            remote(lead, lead, c_send.at[side, slot], c_sem.at[0, 0, 0, 0], "c").wait_send()
+            c_copy(item, side, 0, slot).wait_send()
 
     def x_copy(item, part, source):
         place = source if part == 0 else source // 2
@@ -470,10 +456,10 @@
 
         def one(turn, _):
             here = pl.ds(pl.multiple_of(start + turn * step, 8), step)
-            value = total[side, here].astype(jnp.float32)
+            value = total[side, here]
             for other in others:
                 value = value + other(turn * step, step)
-            total[side, here] = value.astype(jnp.bfloat16)
+            total[side, here] = value
             return 0
 
         lax.fori_loop(0, piece[item] // step, one, 0)
@@ -483,12 +469,12 @@
 
         def read(at, step):
             here = pl.ds(pl.multiple_of(start + at, 8), step)
-            return from_c[side, here, pl.ds(0, width[item])].astype(jnp.float32)
+            return from_c[side, here, pl.ds(0, width[item])]
 
         return read
 
     def of(ref, *place):
-        return lambda at, step: ref[(*place, pl.ds(pl.multiple_of(at, 8), step))].astype(jnp.float32)
+        return lambda at, step: ref[(*place, pl.ds(pl.multiple_of(at, 8), step))]
 
     def mirror(source):
         return source + 1 - 2 * (source % 2)
@@ -501,17 +487,8 @@
         source = target(turn)
         if item > 0:
             pl.semaphore_wait(free_sem, 1)
-        for part, side, place in (
-            (0, 1, source),
-            (1, 1, mirror(source)),
-            (0, 1, mirror(source)),
-            (1, 0, mirror(source)),
-            (0, 0, mirror(source)),
-            (1, 1, source),
-            (0, 0, source),
-            (1, 0, source),
-        ):
-            c_copy(item, part, side, place, turn % 2).start()
+        for side in (1, 0):
+            c_copy(item, side, source, turn % 2).start()
 
     def make(item, turn):
         if 4 * item + turn >= 2:
@@ -520,21 +497,23 @@
         rows = pl.ds(pl.multiple_of(target(turn) // 2 * block, 16), block)
         for quarter in range(4):
             if turn == 0:
-                load(item, quarter).wait()
-            for left, base, span_width, step in layout[item]:
+                for which in range(len(wide_refs[item])):
+                    load(item, quarter, which).wait()
+            for left, base, span_width, step in layout[item][1]:
 
                 def one(chunk, _):
                     at = pl.ds(pl.multiple_of(base + chunk * step, 128), step)
                     found = jnp.dot(
                         lefts[left][rows], rights[quarter, :, at], preferred_element_type=jnp.float32
                     )
-                    if item == 0:
-                        spots = lax.broadcasted_iota(jnp.int32, (places.shape[0], step), 1) + chunk * step
+                    if layout[item][0] is not None:
+                        spots = lax.broadcasted_iota(jnp.int32, (places.shape[0], step), 1)
+                        spots = spots + (layout[item][0] + chunk * step)
                         hot = jnp.where(places[:, quarter : quarter + 1] == spots, 1.0, 0.0)
                         found += jnp.dot(
                             lefts[1][rows], hot.astype(jnp.bfloat16), preferred_element_type=jnp.float32
                         )
-                    if item == gains_at[0] and base == 0:
+                    if extra is not None and item == gains_at[0] and base == 0:
                         found += extra[rows]
                     if quarter % 2:
                         crossed[quarter // 2, turn % 2, :, at] = found.astype(jnp.bfloat16)
@@ -544,28 +523,25 @@
 
                 lax.fori_loop(0, span_width // step, one, 0)
         if turn == 3 and item + 1 < items:
-            for quarter in range(4):
-                load(item + 1, quarter).start()
+            start_loads(item + 1)
 
     def first(item, turn):
         source = target(turn)
+        for side in (1, 0):
+            c_copy(item, side, source).wait_recv()
         for x_place, y_side in ((source, 1), (mirror(source), 0)):
-            c_wait(item, 0, 1, x_place)
             add(item, 1, 0, x_place, c_part(item, 1, 0, x_place))
             x_copy(item, 0, x_place).start()
             y_place = mirror(source)
-            c_wait(item, 1, y_side, y_place)
             add(item, y_side, 1, y_place, c_part(item, y_side, 1, y_place))
             y_copy(item, 1, y_side, y_place).start()
 
     def second(item, turn):
         source = target(turn)
         place = mirror(source)
-        c_wait(item, 0, 0, place)
         x_copy(item, 0, place).wait_recv()
         add(item, 0, 0, place, c_part(item, 0, 0, place), of(held[item][1], place))
         y_copy(item, 0, 0, place).start()
-        c_wait(item, 1, 1, source)
         y_copy(item, 1, 1, source).wait_recv()
         add(item, 1, 1, source, c_part(item, 1, 1, source), of(held[item][4], 1, source // 2))
         x_copy(item, 1, source).start()
@@ -573,7 +549,6 @@
     def third(item, turn):
         source = target(turn)
         for part in range(2):
-            c_wait(item, part, 0, source)
             x_copy(item, part, source).wait_recv()
             y_copy(item, part, 0, source).wait_recv()
             if part == 0:
@@ -618,7 +593,7 @@
                 value = value + jnp.where(z > 0, below, 0.0) + jnp.where(z < 3, above, 0.0)
                 outs[item][pl.ds(pl.multiple_of(part * piece[item] + at, 8), 16)] = value
                 square_here = value * value
-                if item == gains_at[0]:
+                if extra is not None and item == gains_at[0]:
                     lane = lax.broadcasted_iota(jnp.int32, value.shape, 1)
                     repeated = (lane >= gains_at[1]) & (lane < gains_at[1] + gains_at[2])
                     square_here = jnp.where(repeated, square_here / parts, square_here)
@@ -629,9 +604,11 @@
 
     steps = [(item, turn) for item in range(items) for turn in range(4)]
     count = len(steps)
-    make(*steps[0])
-    send_c(*steps[0])
-    for turn in range(count + 3):
+    def begin():
+        make(*steps[0])
+        send_c(*steps[0])
+
+    def advance(turn):
         if turn < count:
             first(*steps[turn])
         if turn + 1 < count:
@@ -643,9 +620,59 @@
             third(*steps[turn - 2])
         if 0 <= turn - 3 < count and (turn - 3) % 4 < 3:
             fourth(*steps[turn - 3])
-    square = sum([last(item) for item in range(items)])
+
+    def finish():
+        return sum([last(item) for item in range(items)])
+
+    def drain():
+        for slot in range(2):
+            c_sent(items - 1, slot)
+        for item in range(items):
+            for way, count in enumerate((12, 12)):
+                lead = held[item][0].at[0, pl.ds(0, count * piece[item])]
+                remote(lead, lead, side_sem.at[way, item], c_sem.at[item, 0, 0], "x").wait_send()
+            for part in range(2):
+                for away in range(3):
+                    pl.when((z < 3) & (z + away + 1 <= 3))(
+                        lambda: z_copy(item, part, column, away, 1).wait_send()
+                    )
+                    pl.when((z > 0) & (z - away - 1 >= 0))(
+                        lambda: z_copy(item, part, column, away, 0).wait_send()
+                    )
+
+    return lambda: start_loads(0), begin, advance, count + 3, finish, drain
+
+
+def reduce_body(layout, parts, gains_at, *refs):
+    table_rights, last_rights = refs[:4], refs[4:8]
+    facts, places, extra = refs[8:11]
+    lefts = refs[11:15]
+    table_out, last_out, totals = refs[15:18]
+    refs = refs[18:]
+    outs, wide_refs = [], []
+    for at, products in layout:
+        span = sum([product[2] for product in products])
+        outs.append(last_out if at is None else table_out.at[:, pl.ds(at, span)])
+        wide_refs.append([(last_rights if at is None else table_rights, at or 0, span)])
+    tile, tile_row, tile_column, row_send, row_recv, column_send, column_recv = refs[:7]
+    start_loads, begin, advance, turns, finish, drain = reduce_tools(
+        layout, gains_at, parts, places, extra, lefts, wide_refs, outs, refs[7:]
+    )
+    start_loads()
+    column = lax.axis_index("dp")
+    row = lax.axis_index("tensor")
+    row_peers = [(column, (row + away) % 4) for away in (1, 2, 3)]
+    column_peers = [((column + away) % 8, row) for away in range(1, 8)]
+    barrier = pltpu.get_barrier_semaphore()
+    for device in row_peers + column_peers:
+        pl.semaphore_signal(barrier, inc=1, device_id=device, device_id_type=MESH)
+    pl.semaphore_wait(barrier, 10)
+    begin()
+    for turn in range(turns):
+        advance(turn)
+    square = finish()
     sublane = lax.broadcasted_iota(jnp.int32, (8, 128), 0)
-    tile[...] = jnp.where(sublane == 0, square, facts[...])
+    tile[...] = facts[...] + jnp.where(sublane == 0, square, 0.0)
 
     def exchange(value, slots, here, peers, sources, send, recv):
         slots[here] = value
@@ -683,53 +710,50 @@
         column_send,
         column_recv,
     )
-    for slot in range(2):
-        c_sent(items - 1, slot)
-    for item in range(items):
-        for way, count in enumerate((12, 12)):
-            lead = held[item][0].at[0, pl.ds(0, count * piece[item])]
-            remote(lead, lead, side_sem.at[way, item], c_sem.at[item, 0, 0, 0], "x").wait_send()
-        for part in range(2):
-            for away in range(3):
-                pl.when((z < 3) & (z + away + 1 <= 3))(
-                    lambda: z_copy(item, part, column, away, 1).wait_send()
-                )
-                pl.when((z > 0) & (z - away - 1 >= 0))(
-                    lambda: z_copy(item, part, column, away, 0).wait_send()
-                )
+    drain()
+
+
+def reduce_scratch(widths, products, rows, depth):
+    whole = lax.axis_size("dp")
+    items, half = len(widths), rows // (2 * whole)
+    scratch = [
+        pltpu.VMEM((*lead, width), jnp.bfloat16)
+        for width in widths
+        for lead in ((2, rows), (8, half), (4, half), (4, half), (2, 4, half), (2, 2, 3, half))
+    ]
+    return scratch + [
+        pltpu.SemaphoreType.DMA((2, items)),
+        pltpu.SemaphoreType.DMA((2, 2)),
+        pltpu.SemaphoreType.DMA((items, 2, 4)),
+        pltpu.SemaphoreType.DMA((items, 2, 8)),
+        pltpu.SemaphoreType.DMA((items, 3, 4)),
+        pltpu.SemaphoreType.DMA((items, 2, 2, 3)),
+        pltpu.SemaphoreType.DMA((items, 2, 2, 3)),
+        pltpu.SemaphoreType.DMA((items, 4, products)),
+        pltpu.SemaphoreType.REGULAR,
+        pltpu.VMEM((2, 2, 4 * half, max(widths)), jnp.bfloat16),
+        pltpu.VMEM((2, rows, max(widths)), jnp.bfloat16),
+        pltpu.VMEM((4, depth, max(widths)), jnp.bfloat16),
+    ]
 
 
 def reduce_kernel(layout, lefts, rights, places, extra, facts, parts, gains_at, tag):
-    items = len(layout)
     anywhere = pl.BlockSpec(memory_space=pl.ANY)
     inside = pl.BlockSpec(memory_space=pltpu.VMEM)
-    whole = lax.axis_size("dp")
     rows, depth = lefts[0].shape
-    half = rows // (2 * whole)
-    widths = [item[0].shape[1] for item in rights]
-    shapes, scratch = [], []
-    for width in widths:
-        shapes.append(jax.ShapeDtypeStruct((rows // whole, width), jnp.float32))
-        for lead in ((2, rows), (8, half), (4, half), (4, half), (2, 4, half), (2, 2, 3, half)):
-            scratch.append(pltpu.VMEM((*lead, width), jnp.bfloat16))
+    widths = [sum([product[2] for product in products]) for _, products in layout]
+    shapes = [
+        jax.ShapeDtypeStruct((rows // lax.axis_size("dp"), item[0].shape[1]), jnp.float32)
+        for item in rights
+    ]
     shapes.append(jax.ShapeDtypeStruct((8, 128), jnp.float32))
     found = pl.pallas_call(
         functools.partial(reduce_body, layout, parts, gains_at),
         name="reduce_grads",
         out_shape=shapes,
-        in_specs=[anywhere] * (4 * items) + [inside] * (3 + len(lefts)),
-        out_specs=[inside] * (items + 1),
-        scratch_shapes=scratch
-        + [
-            pltpu.SemaphoreType.DMA((2, items)),
-            pltpu.SemaphoreType.DMA((2, 2)),
-            pltpu.SemaphoreType.DMA((items, 2, 2, 8)),
-            pltpu.SemaphoreType.DMA((items, 2, 8)),
-            pltpu.SemaphoreType.DMA((items, 3, 4)),
-            pltpu.SemaphoreType.DMA((items, 2, 2, 3)),
-            pltpu.SemaphoreType.DMA((items, 2, 2, 3)),
-            pltpu.SemaphoreType.DMA((items, 4)),
-            pltpu.SemaphoreType.REGULAR,
+        in_specs=[anywhere] * 8 + [inside] * (3 + len(lefts)),
+        out_specs=[inside] * 3,
+        scratch_shapes=[
             pltpu.VMEM((8, 128), jnp.float32),
             pltpu.VMEM((4, 8, 128), jnp.float32),
             pltpu.VMEM((8, 8, 128), jnp.float32),
@@ -737,10 +761,8 @@
             pltpu.SemaphoreType.DMA((4,)),
             pltpu.SemaphoreType.DMA((7,)),
             pltpu.SemaphoreType.DMA((8,)),
-            pltpu.VMEM((2, 2, 4 * half, max(widths)), jnp.bfloat16),
-            pltpu.VMEM((2, rows, max(widths)), jnp.bfloat16),
-            pltpu.VMEM((4, depth, max(widths)), jnp.bfloat16),
-        ],
+        ]
+        + reduce_scratch(widths, 1, rows, depth),
         compiler_params=pltpu.CompilerParams(
             collective_id=tag, has_side_effects=True, vmem_limit_bytes=60 << 20
         ),
@@ -811,12 +833,6 @@
     return tile * cosine + other * sine
 
 
-def greet_core(device):
-    barrier = pltpu.get_barrier_semaphore()
-    pl.semaphore_signal(barrier, inc=1, device_id=device, device_id_type=MESH)
-    pl.semaphore_wait(barrier, 1)
-
-
 def attend_steps(normed, joints, cosine, sine, seg_row, seg_col, packed, lse, attended, between, leaving, heads_out, heads_in, send_sem, recv_sem, out_send, out_recv):
     device = neighbours()["c"]
     rows = normed.shape[0]
@@ -824,7 +840,7 @@
     def project(joint, put):
         found = jnp.dot(normed[...], joint[...], preferred_element_type=jnp.float32)
         for head in range(3):
-            pair = turn_halves(found[:, 192 * head : 192 * head + 128], cosine[...], sine[...])
+            pair = turn_halves(found[:, 192 * head : 192 * head + 128], cosine[0:rows], sine[0:rows])
             value = found[:, 192 * head + 128 : 192 * head + 192]
             put(head, pair.astype(jnp.bfloat16), value.astype(jnp.bfloat16))
 
@@ -860,10 +876,10 @@
 
         def block(turn, _):
             at = pl.ds(pl.multiple_of(turn * 256, 256), 256)
-            query = packed[place, at, 0:128][:, 0:64]
+            query = packed[place, at, 0:128][:, 0:64] * jnp.bfloat16(HEAD_DIM ** (-0.5))
             scores = lax.dot_general(
                 keys, query, (((1,), (1,)), ((), ())), preferred_element_type=jnp.float32
-            ) * HEAD_DIM ** (-0.5)
+            )
             scores = jnp.where(seg_col[:, 0:1] == seg_row[0:1, at], scores, neg_fill)
             top = jnp.max(scores, axis=0, keepdims=True)
             expd = jnp.exp(scores - top)
@@ -905,10 +921,22 @@
         returning(place).wait_send()
 
 
-def attend_back_body(grad_out, packed, lse, attended, cosine, sine, seg_row, seg_col, p0, p1, p2, p3, r0, r1, r2, r3, grads, leaving, keys_t, probs, prob_grads, found, going, coming, send_sem, recv_sem, out_send, out_recv):
+def attend_back_body(layout, *refs):
+    grad_out, packed, lse, attended, cosine, sine, seg_row, seg_col, left_up, left_down = refs[:10]
+    ups, downs = refs[10:14], refs[14:18]
+    p0, p1, p2, p3, r0, r1, r2, r3, summed, square_out = refs[18:28]
+    grads, leaving, keys_t, probs, prob_grads, found, going, coming = refs[28:36]
+    send_sem, recv_sem, out_send, out_recv = refs[36:40]
+    span = ups[0].shape[1]
+    outs = [summed.at[:, pl.ds(0, span)], summed.at[:, pl.ds(span, span)]]
+    wide_refs = [[(ups, 0, span)], [(downs, 0, span)]]
+    start_loads, begin, advance, turns, finish, drain = reduce_tools(
+        layout, None, None, None, None, (left_up, left_down), wide_refs, outs, refs[40:]
+    )
+    start_loads()
     device = neighbours()["c"]
     rows = grad_out.shape[0]
-    greet_core(device)
+    meet(lax.axis_index("dp") // 2, neighbours())
 
     def crossing(place):
         return pltpu.make_async_remote_copy(
@@ -930,11 +958,13 @@
         right[:, 576:640] = nothing
         right[:, 640:832] = attended[:, 192 * order : 192 * order + 192]
         right[:, 832:896] = nothing
+    begin()
     for place in range(6):
         crossing(place).wait_recv()
 
     def one_head(place):
         query = packed[place, :, 0:128][:, 0:64]
+        scaled = query * jnp.bfloat16(HEAD_DIM ** (-0.5))
         wide_keys = packed[place, :, 0:128][:, 64:128].astype(jnp.float32)
         keys_t[...] = wide_keys.T.astype(jnp.bfloat16)
         grad = grads[place, :, 0:64]
@@ -945,8 +975,8 @@
             keys = packed[place, at, 0:128][:, 64:128]
             values = packed[place, at, 128:256][:, 0:64]
             scores = lax.dot_general(
-                keys, query, (((1,), (1,)), ((), ())), preferred_element_type=jnp.float32
-            ) * HEAD_DIM ** (-0.5)
+                keys, scaled, (((1,), (1,)), ((), ())), preferred_element_type=jnp.float32
+            )
             scores = jnp.where(seg_col[at, 0:1] == seg_row[0:1, :], scores, neg_fill)
             prob = jnp.exp(scores - stat)
             prob_grad = lax.dot_general(
@@ -963,8 +993,8 @@
         def spread_back(turn, query_grad):
             at = pl.ds(pl.multiple_of(turn * 256, 256), 256)
             score_grad = (probs[at] * (prob_grads[at] - inner)).astype(jnp.bfloat16)
-            key_grad = jnp.dot(score_grad, query, preferred_element_type=jnp.float32)
-            found[place, at, 64:128] = key_grad * HEAD_DIM ** (-0.5)
+            key_grad = jnp.dot(score_grad, scaled, preferred_element_type=jnp.float32)
+            found[place, at, 64:128] = key_grad
             return query_grad + jnp.dot(keys_t[:, at], score_grad, preferred_element_type=jnp.float32)
 
         query_grad = lax.fori_loop(
@@ -972,11 +1002,13 @@
         )
         found[place, :, 0:64] = query_grad.T * HEAD_DIM ** (-0.5)
 
-    def heads(place, _):
+    for place in range(6):
+        advance(2 * place)
+        if 2 * place + 1 < turns:
+            advance(2 * place + 1)
         one_head(place)
-        return 0
-
-    lax.fori_loop(0, 6, heads, 0)
+    for turn in range(12, turns):
+        advance(turn)
 
     def returning(side):
         return pltpu.make_async_remote_copy(
@@ -1001,6 +1033,7 @@
                     put[:, 192 * head + 128 : 192 * head + 192] = value
             if half:
                 returning(side).start()
+    square_out[...] = jnp.full(square_out.shape, finish(), jnp.float32)
     for side in range(2):
         returning(side).wait_recv()
         for put in ((p1, p3)[side], (r1, r3)[side]):
@@ -1009,18 +1042,25 @@
         crossing(place).wait_send()
     for side in range(2):
         returning(side).wait_send()
-
-
-def attend_back_kernel(grad_out, packed, lse, attended, cosine, sine, seg_row, seg_col):
+    drain()
+
+
+def attend_back_kernel(layout, grad_out, packed, lse, attended, cosine, sine, seg_row, seg_col, lefts, ups, downs):
     rows = grad_out.shape[0]
+    anywhere = pl.BlockSpec(memory_space=pl.ANY)
+    width = ups[0].shape[1] + downs[0].shape[1]
     inside = pl.BlockSpec(memory_space=pltpu.VMEM)
     found = pl.pallas_call(
-        attend_back_body,
+        functools.partial(attend_back_body, layout),
         name="attend_back",
         out_shape=[jax.ShapeDtypeStruct((rows, 640), jnp.bfloat16)] * 4
-        + [jax.ShapeDtypeStruct((rows, 896), jnp.bfloat16)] * 4,
-        in_specs=[inside] * 8,
-        out_specs=[inside] * 8,
+        + [jax.ShapeDtypeStruct((rows, 896), jnp.bfloat16)] * 4
+        + [
+            jax.ShapeDtypeStruct((lefts[0].shape[0] // lax.axis_size("dp"), width), jnp.float32),
+            jax.ShapeDtypeStruct((8, 128), jnp.float32),
+        ],
+        in_specs=[inside] * 10 + [anywhere] * 8,
+        out_specs=[inside] * 10,
         scratch_shapes=[
             pltpu.VMEM((6, 2 * rows, 128), jnp.bfloat16),
             pltpu.VMEM((6, rows, 128), jnp.bfloat16),
@@ -1034,12 +1074,21 @@
             pltpu.SemaphoreType.DMA((6,)),
             pltpu.SemaphoreType.DMA((2,)),
             pltpu.SemaphoreType.DMA((2,)),
-        ],
+        ]
+        + reduce_scratch([width // 2] * 2, 1, *lefts[0].shape),
         compiler_params=pltpu.CompilerParams(
-            collective_id=3, has_side_effects=True, vmem_limit_bytes=56 << 20
+            collective_id=3, has_side_effects=True, vmem_limit_bytes=62 << 20
         ),
-    )(grad_out, packed, lse, attended, cosine, sine, seg_row, seg_col)
-    return found[:4], found[4:]
+    )(grad_out, packed, lse, attended, cosine, sine, seg_row, seg_col, *lefts, *ups, *downs)
+    return found[:4], found[4:8], found[8], found[9]
+
+
+def pieces_of(width):
+    pieces, at = [], 0
+    for span in (768, 640, 640):
+        pieces.append((at, span, span // 2 if span % 256 == 0 else span))
+        at += span
+    return pieces
 
 
 def known_mesh():
@@ -1051,7 +1100,7 @@
         ordered = [[item[0], item[2], item[1], item[3]] for item in rights]
         return reduce_kernel(layout, lefts, ordered, places, extra, facts, parts, gains_at, 1)
     sums = []
-    for item, products in enumerate(layout):
+    for item, (_, products) in enumerate(layout):
         quarters = []
         for quarter, mask in enumerate((0, 2, 1, 3)):
             right = rights[item][quarter]
@@ -1259,10 +1308,8 @@
         return (ids - base)[:, None] == jnp.arange(vocab_part, dtype=jnp.int32)[None, :]
 
     pieces = range(4)
-    places = jnp.pad(
-        jnp.stack([inputs - (place ^ mask) * vocab_part for mask in range(4)], axis=1),
-        ((0, 0), (0, 124)),
-    )
+    lane = jnp.arange(128, dtype=jnp.int32)[None, :]
+    places = inputs[:, None] - (place ^ (lane % 4)) * vocab_part
 
     on_known = known_mesh()
     if on_known:
@@ -1271,7 +1318,7 @@
         seg_row = jnp.broadcast_to(segment[None, :], (8, 2 * rows))
         seg_col = jnp.broadcast_to(segment[:, None], (2 * rows, 128))
         groups, (embedded, normed_one, packed, attn_lse, attended_all) = start_kernel(
-            shards, places, cosines[:rows], sines[:rows], seg_row, seg_col
+            shards, places, cosines, sines, seg_row, seg_col
         )
         groups = [[item[0], item[2], item[1], item[3]] for item in groups]
     else:
@@ -1346,8 +1393,19 @@
     attn_branch = narrow(resid_one)
     attended_grad = narrow(mm(attn_branch, out_all))
     if on_known:
-        proj_grad, last_rights = attend_back_kernel(
-            attended_grad, packed, attn_lse, attended_all, cosines, sines, seg_row, seg_col
+        proj_grad, last_rights, middle_sum, middle_square = attend_back_kernel(
+            ((None, ((0, 0, ff_part, ff_part // 2),)), (None, ((1, 0, ff_part, ff_part // 2),))),
+            attended_grad,
+            packed,
+            attn_lse,
+            attended_all,
+            cosines,
+            sines,
+            seg_row,
+            seg_col,
+            [normed_two.T, mlp_branch.T],
+            [up_input[q] for q in (0, 2, 1, 3)],
+            [activated[q] for q in (0, 2, 1, 3)],
         )
         proj_grad = [proj_grad[q] for q in (0, 2, 1, 3)]
         last_rights = [last_rights[q] for q in (0, 2, 1, 3)]
@@ -1390,24 +1448,29 @@
             jnp.concatenate([fill(proj_grad[q], gains_end), fill(attended_q[q], out_fill)], axis=1)
             for q in range(4)
         ]
-    lefts = [
-        item.T
-        for item in (normed_out, embed_scaled, normed_two, mlp_branch, normed_one, attn_branch)
-    ]
-    rights = [
-        logit_grad,
-        [jnp.concatenate([up_input[q], activated[q]], axis=1) for q in range(4)],
-        last_rights,
-    ]
-    half_ff = ff_part // 2
+    lefts = [normed_out, embed_scaled, normed_one, attn_branch]
+    rights = [logit_grad, last_rights]
     layout = (
-        ((0, 0, vocab_part, 512),),
-        ((2, 0, ff_part, half_ff), (3, ff_part, ff_part, half_ff)),
-        ((4, 0, gains_end, gains_end), (5, gains_end, out_fill, out_fill)),
-    )
+        (None, ((2, 0, gains_end, gains_end), (3, gains_end, out_fill, out_fill))),
+        *((at, ((0, 0, span, step),)) for at, span, step in pieces_of(vocab_part)),
+    )
+    gains_at = (0, head_part, gains_end - head_part)
+    if on_known:
+        facts = facts + jnp.where(sublane == 0, middle_square, 0.0)
+    else:
+        layout = (
+            (0, ((0, 0, vocab_part, vocab_part),)),
+            (None, ((2, 0, gains_end, gains_end), (3, gains_end, out_fill, out_fill))),
+            (None, ((4, 0, ff_part, ff_part), (5, ff_part, ff_part, ff_part))),
+        )
+        gains_at = (1, head_part, gains_end - head_part)
+        lefts = lefts + [normed_two, mlp_branch]
+        rights = rights + [[jnp.concatenate([up_input[q], activated[q]], axis=1) for q in range(4)]]
     sums, totals = reduce_grads(
-        layout, lefts, rights, places, extra, facts, parts, (2, head_part, gains_end - head_part)
-    )
+        layout, [item.T for item in lefts], rights, places, extra, facts, parts, gains_at
+    )
+    if on_known:
+        sums = [*sums, middle_sum]
     step_float = step_count[0].astype(jnp.float32)
     fixes = jnp.where(
         sublane == 0,
@@ -1416,11 +1479,11 @@
     )
     plans = (
         (0, False, 0, rates[0], decays[0]),
-        (2, False, 0, rates[1], decays[1]),
-        (2, True, gains_end, rates[2], decays[2]),
-        (1, False, 0, rates[3], decays[3]),
-        (1, False, ff_part, rates[4], decays[4]),
-        (2, True, head_part, rates[5], decays[5]),
+        (1, False, 0, rates[1], decays[1]),
+        (1, True, gains_end, rates[2], decays[2]),
+        (2, False, 0, rates[3], decays[3]),
+        (2, False, ff_part, rates[4], decays[4]),
+        (1, True, head_part, rates[5], decays[5]),
     )
     triples = (
         (table.T, momentum_table.T, variance_table.T),

time: 453 us -> 444 us (0.980)
  Pallas kernels: 331 us -> 326 us
    pallas_call x1, Pallas kernels: 150 us -> 106 us  [reduce_kernel(): pl.pallas_call(functools.partial(reduce_body, layout, parts, gains_at), n...]
    pallas_call x1, Pallas kernels: 41.7 us -> 79.2 us  [attend_back_kernel(): pl.pallas_call(functools.partial(attend_back_body, layout), name='attend_...]
    concatenate x4 -> x0, other arithmetic: 5.13 us -> none  [per_device(): jnp.concatenate([up_input[q], activated[q]], axis=1)]
    unnamed x139 -> x127, local copies, waits for them, and re-layouts: 15.7 us -> 14.1 us
where the time goes in v1:
time: 444 us; the launch traced here: 440 us
  Pallas kernels  326 us (73%)
  matrix products  48.5 us (11%)
  other arithmetic  37.7 us (8%)
  local copies, waits for them, and re-layouts  23.9 us (5%)
    pallas_call x1, Pallas kernels, start_kernel(): pl.pallas_call(functools.partial(start_body, items), name='start', out_sh...  135 us
    pallas_call x1, Pallas kernels, reduce_kernel(): pl.pallas_call(functools.partial(reduce_body, layout, parts, gains_at), n...  106 us
    pallas_call x1, Pallas kernels, attend_back_kernel(): pl.pallas_call(functools.partial(attend_back_body, layout), name='attend_...  79.2 us
    dot_general x17, matrix products, mm_nt(): lax.dot_general(left, right, (((1,), (1,)), ((), ())), preferred_element_...  25.4 us
    dot_general x13, matrix products, mm(): return jnp.dot(left, right, preferred_element_type=jnp.float32)  23.1 us
    unnamed x127, local copies, waits for them, and re-layouts  14.1 us
    convert_element_type x7, other arithmetic, narrow(): return value.astype(jnp.bfloat16)  10.9 us

profile of v1, /device:TPU:0, one launch (start us, length us, event | category | flops | bytes accessed | tf_op | source)
XLA Modules:
  0.0 439.7 jit_solution(4760021000878341692)
XLA Ops:
  0.7 2.0 convert_bitcast_fusion.2.refs_0_
  12.1 1.9 fusion.27
  14.0 1.3 pad_maximum_fusion.1.refs_6_.refs_4_
  18.1 134.5 %start.1 = (bf16[768,2048]{1,0:T(8,128)(2,1)}, bf16[768,2048]{1,0:T(8,128)(2,1)}, bf16[768,2048]{1,0:T(8,128)(2,1)}, bf16[768,2048]{1,0:T(8,128)(2,1)}, bf16[768...) custom-call(bf16[96,2048]{1,0:T(8,128)(2,1)} %convert_bitcast_fusion, ...), custom_call_target="tpu_custom_call" | custom-call | tf_op jit(solution)/shard_map/start/pallas_call | solution.py:337
  152.7 2.0 copy.147
  154.8 2.5 multiply_reduce_fusion.8
  159.6 2.0 multiply_convert_fusion.6
  161.7 2.1 multiply_convert_fusion.7
  165.4 2.1 multiply_convert_fusion.9
  169.0 2.1 multiply_convert_fusion.8
  175.1 2.0 fusion.37
  177.1 2.2 fusion.40
  179.3 2.0 fusion.38
  181.3 2.0 fusion.39
  183.3 5.0 %select_reduce_fusion.2 = (f32[512]{0:T(512)S(1)}, f32[512]{0:T(512)S(1)}, f32[512]{0:T(512)S(1)}, f32[512]{0:T(512)S(1)}, f32[512]{0:T(512)S(1)}, /*index=5*/f32[512]{0:T(512)S(1)}, f32[512]{0:T(512)S(1)}, f32[512]{0:T(512)S(1)}) fusion(f32[512,2048]{1,0:T(8,128)S(1)} %get-tuple-element.197, s32[512]{0:T(512)S(1)} %get-tuple-element.158, ...), kind=kLoop, calls=%fused_computation.2 | loop fusion | flops 20967424 | bytes 16803840 | tf_op jit(solution)/shard_map/reduce_sum | solution.py:1371
  188.9 7.8 %multiply_convert_fusion = (bf16[512,2048]{1,0:T(8,128)(2,1)S(1)}, bf16[512,2048]{1,0:T(8,128)(2,1)}, bf16[512,2048]{1,0:T(8,128)(2,1)}, bf16[512,2048]{1,0:T(8,128)(2,1)}) fusion(f32[512,2048]{1,0:T(8,128)S(1)} %get-tuple-element.191, s32[512]{0:T(512)S(1)} %get-tuple-element.161, f32[512]{0:T(512)S(1)} %get-tuple-element.155, ...), kind=kLoop, calls=%fused_computation.4 | loop fusion | flops 25165824 | bytes 25178112 | tf_op jit(solution)/shard_map/convert_element_type | solution.py:1127
  196.7 5.1 %fusion.46 = f32[512,768]{0,1:T(8,128)S(1)} fusion(bf16[512,2048]{1,0:T(8,128)(2,1)} %get-tuple-element.170.refs_1_, bf16[768,2048]{1,0:T(8,128)(2,1)} %get-tuple-element.94), kind=kOutput, calls=%fused_computation.144 | convolution fusion | flops 1610612736 | bytes 6815744 | tf_op jit(solution)/shard_map/dot_general | solution.py:1167
  201.9 1.8 fusion.44
  203.7 1.8 fusion.45
  205.6 2.3 multiply_reduce_fusion.1
  218.3 1.4 fusion.11.refs_12_
  221.8 1.3 multiply_reduce_fusion.2
  223.2 1.7 convert_bitcast_fusion.1
  224.9 1.9 convolution_convert_fusion.refs_0_
  227.8 79.2 %attend_back.1 = (bf16[512,640]{1,0:T(8,128)(2,1)}, bf16[512,640]{1,0:T(8,128)(2,1)}, bf16[512,640]{1,0:T(8,128)(2,1)}, bf16[512,640]{1,0:T(8,128)(2,1)}, bf16[5...) custom-call(bf16[512,768]{1,0:T(8,128)(2,1)} %convolution_convert_fu, ...), custom_call_target="tpu_custom_call" | custom-call | tf_op jit(solution)/shard_map/attend_back/pallas_call | solution.py:1053
  307.9 2.0 select_add_fusion.refs_8_
  309.9 1.6 multiply_reduce_fusion.4
  316.1 2.3 multiply_reduce_fusion
  318.6 1.6 pad.9.refs_10_
  322.1 1.4 fusion.24.refs_12_
  324.6 106.2 %reduce_grads.1 = (f32[96,2048]{1,0:T(8,128)}, f32[96,896]{1,0:T(8,128)}, f32[8,128]{1,0:T(8,128)}) custom-call(bf16[512,2048]{1,0:T(8,128)(2,1)} %get-tuple-element.171.refs_0_, bf16[512,2048]{1,0:T(8,128)(2,1)} %get-tuple-element.170.refs_1_, bf16[512,2048]{1,0:T(8,128)(2,1)} %get-tuple-element.169.refs_2_, bf16[512,2048]{1,0:T(8,128)(2,1)} %copy-done.8, ...), custom_call_target="tpu_custom_call" | custom-call | tf_op jit(solution)/shard_map/reduce_grads/pallas_call | solution.py:750
  432.3 5.8 %update_weights.1 = (f32[96,2048]{1,0:T(8,128)}, f32[96,2048]{1,0:T(8,128)}, f32[96,2048]{1,0:T(8,128)}, f32[96,576]{1,0:T(8,128)}, f32[96,576]{1,0:T(8,128)}, /...) custom-call(f32[8,128]{1,0:T(8,128)} %get-tuple-element.111.refs_0_,, ...), custom_call_target="tpu_custom_call" | custom-call | tf_op jit(solution)/shard_map/update_weights/pallas_call | solution.py:819
  (190 shorter events, 45.2 us)
Async XLA Ops:
  0.7 4.5 %copy-start.18 = (f32[96,768]{1,0:T(8,128)S(1)}, f32[96,768]{1,0:T(8,128)}, u32[]{:S(2)}) copy-start(f32[96,768]{1,0:T(8,128)} %refs_14_.1) | copy-start | bytes 884740
  0.7 5.2 %copy-start.19 = (f32[768,96]{0,1:T(8,128)S(1)}, f32[768,96]{0,1:T(8,128)}, u32[]{:S(2)}) copy-start(f32[768,96]{0,1:T(8,128)} %param.32) | copy-start | bytes 884740
  0.7 5.9 %copy-start.39 = (f32[192,96]{1,0:T(8,128)S(1)}, f32[192,96]{1,0:T(8,128)}, u32[]{:S(2)}) copy-start(f32[192,96]{1,0:T(8,128)} %refs_11_.1) | copy-start | bytes 221188
  0.7 6.6 %copy-start.40 = (s32[2,4]{1,0:T(2,128)S(1)}, s32[2,4]{1,0:T(2,128)}, u32[]{:S(2)}) copy-start(s32[2,4]{1,0:T(2,128)} %param.24) | copy-start | bytes 100
  0.7 6.9 %copy-start.58 = (s32[2]{0:T(128)S(1)}, s32[2]{0:T(128)}, u32[]{:S(2)}) copy-start(s32[2]{0:T(128)} %param.25) | copy-start | bytes 28
  152.7 2.0 copy-start.27
  152.7 2.0 copy-start.53
  152.7 2.0 copy-start.54
  154.7 2.6 copy-start
  159.6 2.1 copy-start.49
  161.7 11.1 %copy-start.15 = (bf16[512,768]{1,0:T(8,128)(2,1)}, bf16[512,768]{1,0:T(8,128)(2,1)S(1)}, u32[]{:S(2)}) copy-start(bf16[512,768]{1,0:T(8,128)(2,1)S(1)} %get-tuple-element.186.refs_17_) | copy-start | bytes 2359300
  161.7 2.1 copy-start.51
  165.4 2.1 copy-start.47
  169.0 2.9 copy-start.43
  173.2 1.9 copy-start.3
  175.1 2.0 copy-start.4
  177.1 2.2 copy-start.7
  179.3 2.0 copy-start.5
  196.7 8.8 %copy-start.8 = (bf16[512,2048]{1,0:T(8,128)(2,1)}, bf16[512,2048]{1,0:T(8,128)(2,1)S(1)}, u32[]{:S(2)}) copy-start(bf16[512,2048]{1,0:T(8,128)(2,1)S(1)} %get-tuple-element.168.refs_3_) | copy-start | bytes 6291460
  196.7 5.2 %copy-start.6 = (bf16[768,2048]{1,0:T(8,128)(2,1)S(1)}, bf16[768,2048]{1,0:T(8,128)(2,1)}, u32[]{:S(2)}) copy-start(bf16[768,2048]{1,0:T(8,128)(2,1)} %get-tuple-element.92) | copy-start | bytes 9437188
  196.7 5.2 %copy-start.10 = (bf16[512,2048]{1,0:T(8,128)(2,1)S(1)}, bf16[512,2048]{1,0:T(8,128)(2,1)}, u32[]{:S(2)}) copy-start(bf16[512,2048]{1,0:T(8,128)(2,1)} %get-tuple-element.171.refs_0_) | copy-start | bytes 6291460
  209.6 7.5 %copy-start.14 = (bf16[512,768]{0,1:T(8,128)(2,1)}, bf16[512,768]{0,1:T(8,128)(2,1)S(1)}, u32[]{:S(2)}) copy-start(bf16[512,768]{0,1:T(8,128)(2,1)S(1)} %fusion.35) | copy-start | bytes 2359300
  209.6 2.0 copy-start.61
  210.8 10.6 %copy-start.16 = (bf16[512,768]{1,0:T(8,128)(2,1)}, bf16[512,768]{1,0:T(8,128)(2,1)S(1)}, u32[]{:S(2)}) copy-start(bf16[512,768]{1,0:T(8,128)(2,1)S(1)} %fusion.23.refs_13_) | copy-start | bytes 2359300
  212.9 2.0 copy-start.60
  216.3 2.0 copy-start.59
  218.3 2.3 copy-start.42
  307.1 4.4 %copy-start.26 = (bf16[768,640]{1,0:T(8,128)(2,1)S(1)}, bf16[768,640]{1,0:T(8,128)(2,1)}, u32[]{:S(2)}) copy-start(bf16[768,640]{1,0:T(8,128)(2,1)} %get-tuple-element.107) | copy-start | bytes 2949124
  307.1 4.4 %copy-start.38 = (bf16[512,640]{1,0:T(8,128)(2,1)S(1)}, bf16[512,640]{1,0:T(8,128)(2,1)}, u32[]{:S(2)}) copy-start(bf16[512,640]{1,0:T(8,128)(2,1)} %get-tuple-element.106) | copy-start | bytes 1966084
  318.6 2.7 copy-start.11
  318.6 2.7 copy-start.13
  320.2 1.9 copy-start.2
  (31 other events, 42.7 us)

commit v2 on v1

--- a/solution.py
+++ b/solution.py
@@ -110,36 +110,44 @@
 
 
 def start_body(items, *refs):
-    ins = refs[:items]
-    places, cosine, sine, seg_row, seg_col = refs[items : items + 5]
-    refs = refs[items + 5 :]
-    outs = [refs[4 * item : 4 * item + 4] for item in range(items)]
-    embedded_out, normed, packed, lse, attended = refs[4 * items : 4 * items + 5]
-    refs = refs[4 * items + 5 :]
-    side_sem, z_sem, recv_sem, own_sem, keep_sem = refs[:5]
-    staged = refs[5:7]
-    attend_refs = refs[7:]
+    arrays = items - 1
+    given = refs[:arrays]
+    places, cosine, sine, seg_row, seg_col = refs[arrays : arrays + 5]
+    refs = refs[arrays + 5 :]
+    kept = [refs[4 * array : 4 * array + 4] for array in range(arrays)]
+    embedded_out, normed, packed, lse, attended = refs[4 * arrays : 4 * arrays + 5]
+    refs = refs[4 * arrays + 5 :]
+    side_sem, z_sem, late_sem, recv_sem, own_sem, keep_sem = refs[:6]
+    staged = refs[6:8]
+    attend_refs = refs[8:]
+    late = (1, 3)
+    cut = given[0].shape[1] - 256
+    columns = [pl.ds(0, cut), pl.ds(cut, 256)] + [pl.ds(0, item.shape[1]) for item in given[1:]]
+    ins = [given[0].at[:, columns[0]], given[0].at[:, columns[1]], *given[1:]]
     column = lax.axis_index("dp")
     z = column // 2
     devices = neighbours()
     meet(z, devices)
-    shard = [item.shape[0] for item in ins]
+    shard = [given[0].shape[0]] * items
     piece = [item // 2 for item in shard]
 
-    def base(item, quarter):
-        return staged[item].at[quarter] if item < 2 else outs[item][quarter]
+    def base(item, quarter, rows):
+        if item < 3:
+            return staged[item // 2].at[quarter, rows, columns[item]]
+        return kept[item - 1][quarter].at[rows]
 
     def mirror(source):
         return source + 1 - 2 * (source % 2)
 
     def view(item, part, quarter, source):
         start = pl.multiple_of(source * shard[item] + part * piece[item], 8)
-        return base(item, quarter).at[pl.ds(start, piece[item])]
+        return base(item, quarter, pl.ds(start, piece[item]))
 
     def copy(item, part, quarter, source, to_quarter, name, send, own=False):
         here = view(item, part, quarter, source)
         if own:
-            here = ins[item].at[pl.ds(part * piece[item], piece[item])]
+            own_rows = pl.ds(part * piece[item], piece[item])
+            here = given[0].at[own_rows, columns[item]] if item < 2 else given[item - 1].at[own_rows]
         return pltpu.make_async_remote_copy(
             src_ref=here,
             dst_ref=view(item, part, to_quarter, source),
@@ -161,9 +169,12 @@
     def send_c(item, part, quarter, source, own=False):
         copy(item, part, quarter, source, quarter + 1, "c", side_sem.at[2 + quarter // 2, item], own).start()
 
-    def send_z(item, part, source, turn, upward, own=False):
+    def send_z(item, part, source, turn, upward, own=False, quarter=0, kind=0):
         name = "up" if upward else "down"
-        copy(item, part, 0, source, 0, name, z_sem.at[item, part, 1 - upward, turn], own).start()
+        sem = z_sem.at[item, part, 1 - upward, turn]
+        if item in late:
+            sem = late_sem.at[item // 2, part, 1 - upward, turn, kind]
+        copy(item, part, quarter, source, quarter, name, sem, own).start()
 
     def slot(turn, action):
         pl.when(z >= turn)(lambda: action(column - 2 * turn, 1))
@@ -174,12 +185,12 @@
     def local(item):
         return pltpu.make_async_copy(
             ins[item],
-            base(item, 0).at[pl.ds(pl.multiple_of(column * shard[item], 8), shard[item])],
+            base(item, 0, pl.ds(pl.multiple_of(column * shard[item], 8), shard[item])),
             own_sem.at[item],
         )
 
     def keep(item, quarter):
-        return pltpu.make_async_copy(staged[item].at[quarter], outs[item][quarter], keep_sem.at[item, quarter])
+        return pltpu.make_async_copy(staged[item].at[quarter], kept[item][quarter], keep_sem.at[item, quarter])
 
     def begin(item):
         for part in range(2):
@@ -232,24 +243,71 @@
                 for quarter in (1, 3):
                     arrived(item, part, quarter, source)
         local(item).wait()
-        if item < 2:
+        if item in (1, 2):
             for quarter in range(4):
-                keep(item, quarter).start()
-
-    rest = range(2, items)
+                keep(item - 1, quarter).start()
+
+    def kinds(source):
+        return ((0, source), (2, source), (0, mirror(source)), (2, mirror(source)))
+
+    def both_ways(item, part, kind):
+        quarter, source = kinds(column)[kind]
+        pl.when(z < 3)(lambda: send_z(item, part, source, 0, 1, False, quarter, kind))
+        pl.when(z > 0)(lambda: send_z(item, part, source, 0, 0, False, quarter, kind))
+        send_c(item, part, quarter, source)
+
+    def late_first(item):
+        other = mirror(column)
+        arrived(item, 0, 2, column)
+        send_y(item, 0, 2, column)
+        both_ways(item, 0, 1)
+        arrived(item, 1, 0, other)
+        send_x(item, 1, other)
+        both_ways(item, 1, 2)
+        arrived(item, 0, 0, other)
+        both_ways(item, 0, 2)
+        arrived(item, 1, 2, column)
+        both_ways(item, 1, 1)
+
+    def late_second(item):
+        for part in range(2):
+            arrived(item, part, 2, mirror(column))
+            both_ways(item, part, 3)
+
+    def late_z(item, turn):
+        def action(place, upward):
+            for kind, (quarter, source) in enumerate(kinds(place)):
+                for part in range(2):
+                    arrived(item, part, quarter, source)
+                    if turn < 3:
+                        ahead = z < 3 if upward else z > 0
+                        pl.when(ahead)(lambda: send_z(item, part, source, turn, upward, False, quarter, kind))
+                    send_c(item, part, quarter, source)
+
+        slot(turn, action)
+
+    rest = range(4, items)
     begin(0)
-    for turn in (1, 2, 3):
+    begin(1)
+    late_first(1)
+    along_z(0, 1)
+    late_second(1)
+    for turn in (2, 3):
         along_z(0, turn)
-    begin(1)
+    late_z(1, 1)
+    begin(2)
     for turn in range(4):
         onward(second, 0, turn)
+    late_z(1, 2)
     for turn in (1, 2, 3):
-        along_z(1, turn)
+        along_z(2, turn)
+    late_z(1, 3)
     for turn in range(4):
         onward(third, 0, turn)
-    for item in rest:
+    for item in range(3, items):
         begin(item)
     complete(0)
+    complete(1)
 
     def look_up(quarter):
         def one(chunk, _):
@@ -265,18 +323,21 @@
 
     embedded_out[...] = jnp.zeros_like(embedded_out)
     look_up(0)
+    late_first(3)
     for turn in range(4):
-        onward(second, 1, turn)
+        onward(second, 2, turn)
     look_up(2)
     for item in rest:
         along_z(item, 1)
+    late_second(3)
     look_up(1)
     for turn in range(4):
-        onward(third, 1, turn)
+        onward(third, 2, turn)
     for item in rest:
         along_z(item, 2)
+    late_z(3, 1)
     look_up(3)
-    complete(1)
+    complete(2)
     gain = staged[1][0, :, 512:640].astype(jnp.float32).T[64:65]
     value = embedded_out[...] * D**0.5
     embedded_out[...] = value
@@ -286,6 +347,8 @@
         along_z(item, 3)
 
     def between(stage):
+        if stage in (2, 5):
+            late_z(3, 2 if stage == 2 else 3)
         for item in rest:
             if stage == 0:
                 onward(second, item, 0)
@@ -293,22 +356,21 @@
             if stage == 1:
                 onward(second, item, 2)
                 onward(second, item, 3)
-            if stage in (3, 4, 5):
-                onward(third, item, (0, 1, 2)[stage - 3])
             if stage == 6:
-                onward(third, item, 3)
+                for turn in range(4):
+                    onward(third, item, turn)
 
     attend_steps(
         normed, [staged[1].at[q] for q in range(4)], cosine, sine, seg_row, seg_col, packed, lse, attended, between, *attend_refs
     )
-    for item in rest:
+    for item in range(3, items):
         complete(item)
     for item in range(2):
         for quarter in range(4):
             keep(item, quarter).wait()
     for item in range(items):
-        for way, count in enumerate((12, 12, 16, 16)):
-            lead = base(item, 0).at[pl.ds(0, count * piece[item])]
+        for way, count in enumerate((3, 3, 16, 16) if item in late else (12, 12, 16, 16)):
+            lead = base(item, 0, pl.ds(0, count * piece[item]))
             pltpu.make_async_remote_copy(
                 src_ref=lead,
                 dst_ref=lead,
@@ -319,16 +381,22 @@
             ).wait_send()
     for item, part in every:
         for turn in range(3):
-            pl.when((z < 3) & (z >= turn))(
-                lambda: copy(item, part, 0, column, 0, "up", z_sem.at[item, part, 0, turn], True).wait_send()
-            )
-            pl.when((z > 0) & (z + turn <= 3))(
-                lambda: copy(item, part, 0, column, 0, "down", z_sem.at[item, part, 1, turn], True).wait_send()
-            )
+            for kind in range(4 if item in late else 1):
+                sems = [
+                    late_sem.at[item // 2, part, way, turn, kind] if item in late else z_sem.at[item, part, way, turn]
+                    for way in range(2)
+                ]
+                pl.when((z < 3) & (z >= turn))(
+                    lambda: copy(item, part, 0, column, 0, "up", sems[0], True).wait_send()
+                )
+                pl.when((z > 0) & (z + turn <= 3))(
+                    lambda: copy(item, part, 0, column, 0, "down", sems[1], True).wait_send()
+                )
 
 
 def start_kernel(shards, places, cosine, sine, seg_row, seg_col):
-    items = len(shards)
+    arrays = len(shards)
+    items = arrays + 1
     anywhere = pl.BlockSpec(memory_space=pl.ANY)
     inside = pl.BlockSpec(memory_space=pltpu.VMEM)
     whole, rows = lax.axis_size("dp"), places.shape[0]
@@ -345,11 +413,12 @@
             jax.ShapeDtypeStruct((8, 2 * rows), jnp.float32),
             jax.ShapeDtypeStruct((rows, 768), jnp.bfloat16),
         ],
-        in_specs=[anywhere] * items + [inside] * 5,
-        out_specs=[anywhere] * (4 * items) + [inside] * 5,
+        in_specs=[anywhere] * arrays + [inside] * 5,
+        out_specs=[anywhere] * (4 * arrays) + [inside] * 5,
         scratch_shapes=[
             pltpu.SemaphoreType.DMA((4, items)),
             pltpu.SemaphoreType.DMA((items, 2, 2, 3)),
+            pltpu.SemaphoreType.DMA((2, 2, 2, 3, 4)),
             pltpu.SemaphoreType.DMA((items, 2, 4, 8)),
             pltpu.SemaphoreType.DMA((items,)),
             pltpu.SemaphoreType.DMA((2, 4)),
@@ -367,7 +436,7 @@
             collective_id=0, has_side_effects=True, vmem_limit_bytes=56 << 20
         ),
     )(*shards, places, cosine, sine, seg_row, seg_col)
-    return [flat[4 * item : 4 * item + 4] for item in range(items)], flat[4 * items :]
+    return [flat[4 * array : 4 * array + 4] for array in range(arrays)], flat[4 * arrays :]
 
 
 def reduce_tools(layout, gains_at, parts, places, extra, lefts, wide_refs, outs, refs):
@@ -1085,7 +1154,7 @@
 
 def pieces_of(width):
     pieces, at = [], 0
-    for span in (768, 640, 640):
+    for span in (1024, 1024):
         pieces.append((at, span, span // 2 if span % 256 == 0 else span))
         at += span
     return pieces

time: 444 us -> 442 us (level)
  no operation moved by 1% of the time
where the time goes in v2:
time: 442 us; the launch traced here: 436 us
  Pallas kernels  322 us (73%)
  matrix products  48.5 us (11%)
  other arithmetic  37.8 us (9%)
  local copies, waits for them, and re-layouts  23.9 us (5%)
    pallas_call x1, Pallas kernels, start_kernel(): pl.pallas_call(functools.partial(start_body, items), name='start', out_sh...  132 us
    pallas_call x1, Pallas kernels, reduce_kernel(): pl.pallas_call(functools.partial(reduce_body, layout, parts, gains_at), n...  107 us
    pallas_call x1, Pallas kernels, attend_back_kernel(): pl.pallas_call(functools.partial(attend_back_body, layout), name='attend_...  77.1 us
    dot_general x17, matrix products, mm_nt(): lax.dot_general(left, right, (((1,), (1,)), ((), ())), preferred_element_...  25.4 us
    dot_general x13, matrix products, mm(): return jnp.dot(left, right, preferred_element_type=jnp.float32)  23.1 us
    unnamed x127, local copies, waits for them, and re-layouts  14.1 us
    convert_element_type x7, other arithmetic, narrow(): return value.astype(jnp.bfloat16)  11 us

profile of v2, /device:TPU:0, one launch (start us, length us, event | category | flops | bytes accessed | tf_op | source)
XLA Modules:
  0.0 435.8 jit_solution(6712354580492718399)
XLA Ops:
  0.7 2.0 convert_bitcast_fusion.2.refs_0_
  12.1 1.9 fusion.27
  14.0 1.3 pad_maximum_fusion.1.refs_6_.refs_4_
  18.1 132.1 %start.1 = (bf16[768,2048]{1,0:T(8,128)(2,1)}, bf16[768,2048]{1,0:T(8,128)(2,1)}, bf16[768,2048]{1,0:T(8,128)(2,1)}, bf16[768,2048]{1,0:T(8,128)(2,1)}, bf16[768...) custom-call(bf16[96,2048]{1,0:T(8,128)(2,1)} %convert_bitcast_fusion, ...), custom_call_target="tpu_custom_call" | custom-call | tf_op jit(solution)/shard_map/start/pallas_call | solution.py:405
  150.3 2.0 copy.147
  152.3 2.5 multiply_reduce_fusion.8
  157.2 2.0 multiply_convert_fusion.6
  159.2 2.1 multiply_convert_fusion.7
  162.9 2.1 multiply_convert_fusion.9
  166.6 2.1 multiply_convert_fusion.8
  172.7 2.0 fusion.37
  174.7 2.2 fusion.40
  176.9 2.0 fusion.38
  178.9 2.0 fusion.39
  180.9 5.0 %select_reduce_fusion.2 = (f32[512]{0:T(512)S(1)}, f32[512]{0:T(512)S(1)}, f32[512]{0:T(512)S(1)}, f32[512]{0:T(512)S(1)}, f32[512]{0:T(512)S(1)}, /*index=5*/f32[512]{0:T(512)S(1)}, f32[512]{0:T(512)S(1)}, f32[512]{0:T(512)S(1)}) fusion(f32[512,2048]{1,0:T(8,128)S(1)} %get-tuple-element.197, s32[512]{0:T(512)S(1)} %get-tuple-element.158, ...), kind=kLoop, calls=%fused_computation.2 | loop fusion | flops 20967424 | bytes 16803840 | tf_op jit(solution)/shard_map/reduce_sum | solution.py:1440
  186.4 7.9 %multiply_convert_fusion = (bf16[512,2048]{1,0:T(8,128)(2,1)S(1)}, bf16[512,2048]{1,0:T(8,128)(2,1)}, bf16[512,2048]{1,0:T(8,128)(2,1)}, bf16[512,2048]{1,0:T(8,128)(2,1)}) fusion(f32[512,2048]{1,0:T(8,128)S(1)} %get-tuple-element.191, s32[512]{0:T(512)S(1)} %get-tuple-element.161, f32[512]{0:T(512)S(1)} %get-tuple-element.155, ...), kind=kLoop, calls=%fused_computation.4 | loop fusion | flops 25165824 | bytes 25178112 | tf_op jit(solution)/shard_map/convert_element_type | solution.py:1196
  194.4 5.1 %fusion.46 = f32[512,768]{0,1:T(8,128)S(1)} fusion(bf16[512,2048]{1,0:T(8,128)(2,1)} %get-tuple-element.170.refs_1_, bf16[768,2048]{1,0:T(8,128)(2,1)} %get-tuple-element.94), kind=kOutput, calls=%fused_computation.144 | convolution fusion | flops 1610612736 | bytes 6815744 | tf_op jit(solution)/shard_map/dot_general | solution.py:1236
  199.5 1.8 fusion.44
  201.4 1.8 fusion.45
  203.2 2.3 multiply_reduce_fusion.1
  215.9 1.4 fusion.11.refs_12_
  219.5 1.3 multiply_reduce_fusion.2
  220.8 1.7 convert_bitcast_fusion.1
  222.5 1.9 convolution_convert_fusion.refs_0_
  225.5 77.1 %attend_back.1 = (bf16[512,640]{1,0:T(8,128)(2,1)}, bf16[512,640]{1,0:T(8,128)(2,1)}, bf16[512,640]{1,0:T(8,128)(2,1)}, bf16[512,640]{1,0:T(8,128)(2,1)}, bf16[5...) custom-call(bf16[512,768]{1,0:T(8,128)(2,1)} %convolution_convert_fu, ...), custom_call_target="tpu_custom_call" | custom-call | tf_op jit(solution)/shard_map/attend_back/pallas_call | solution.py:1122
  303.4 2.0 select_add_fusion.refs_8_
  305.4 1.6 multiply_reduce_fusion.4
  311.6 2.3 multiply_reduce_fusion
  314.1 1.6 pad.9.refs_10_
  317.6 1.4 fusion.24.refs_12_
  320.1 106.9 %reduce_grads.1 = (f32[96,2048]{1,0:T(8,128)}, f32[96,896]{1,0:T(8,128)}, f32[8,128]{1,0:T(8,128)}) custom-call(bf16[512,2048]{1,0:T(8,128)(2,1)} %get-tuple-element.171.refs_0_, bf16[512,2048]{1,0:T(8,128)(2,1)} %get-tuple-element.170.refs_1_, bf16[512,2048]{1,0:T(8,128)(2,1)} %get-tuple-element.169.refs_2_, bf16[512,2048]{1,0:T(8,128)(2,1)} %copy-done.8, ...), custom_call_target="tpu_custom_call" | custom-call | tf_op jit(solution)/shard_map/reduce_grads/pallas_call | solution.py:819
  428.5 5.8 %update_weights.1 = (f32[96,2048]{1,0:T(8,128)}, f32[96,2048]{1,0:T(8,128)}, f32[96,2048]{1,0:T(8,128)}, f32[96,576]{1,0:T(8,128)}, f32[96,576]{1,0:T(8,128)}, /...) custom-call(f32[8,128]{1,0:T(8,128)} %get-tuple-element.111.refs_0_,, ...), custom_call_target="tpu_custom_call" | custom-call | tf_op jit(solution)/shard_map/update_weights/pallas_call | solution.py:888
  (190 shorter events, 45.2 us)
Async XLA Ops:
  0.7 4.5 %copy-start.18 = (f32[96,768]{1,0:T(8,128)S(1)}, f32[96,768]{1,0:T(8,128)}, u32[]{:S(2)}) copy-start(f32[96,768]{1,0:T(8,128)} %refs_14_.1) | copy-start | bytes 884740
  0.7 5.2 %copy-start.19 = (f32[768,96]{0,1:T(8,128)S(1)}, f32[768,96]{0,1:T(8,128)}, u32[]{:S(2)}) copy-start(f32[768,96]{0,1:T(8,128)} %param.32) | copy-start | bytes 884740
  0.7 5.9 %copy-start.39 = (f32[192,96]{1,0:T(8,128)S(1)}, f32[192,96]{1,0:T(8,128)}, u32[]{:S(2)}) copy-start(f32[192,96]{1,0:T(8,128)} %refs_11_.1) | copy-start | bytes 221188
  0.7 6.6 %copy-start.40 = (s32[2,4]{1,0:T(2,128)S(1)}, s32[2,4]{1,0:T(2,128)}, u32[]{:S(2)}) copy-start(s32[2,4]{1,0:T(2,128)} %param.24) | copy-start | bytes 100
  0.7 6.9 %copy-start.58 = (s32[2]{0:T(128)S(1)}, s32[2]{0:T(128)}, u32[]{:S(2)}) copy-start(s32[2]{0:T(128)} %param.25) | copy-start | bytes 28
  150.3 2.0 copy-start.27
  150.3 2.0 copy-start.53
  150.3 2.0 copy-start.54
  152.3 2.6 copy-start
  157.2 2.1 copy-start.49
  159.2 11.1 %copy-start.15 = (bf16[512,768]{1,0:T(8,128)(2,1)}, bf16[512,768]{1,0:T(8,128)(2,1)S(1)}, u32[]{:S(2)}) copy-start(bf16[512,768]{1,0:T(8,128)(2,1)S(1)} %get-tuple-element.186.refs_17_) | copy-start | bytes 2359300
  159.2 2.1 copy-start.51
  162.9 2.1 copy-start.47
  166.6 2.9 copy-start.43
  170.8 1.9 copy-start.3
  172.7 2.0 copy-start.4
  174.6 2.2 copy-start.7
  176.9 2.0 copy-start.5
  194.3 8.9 %copy-start.8 = (bf16[512,2048]{1,0:T(8,128)(2,1)}, bf16[512,2048]{1,0:T(8,128)(2,1)S(1)}, u32[]{:S(2)}) copy-start(bf16[512,2048]{1,0:T(8,128)(2,1)S(1)} %get-tuple-element.168.refs_3_) | copy-start | bytes 6291460
  194.3 5.2 %copy-start.6 = (bf16[768,2048]{1,0:T(8,128)(2,1)S(1)}, bf16[768,2048]{1,0:T(8,128)(2,1)}, u32[]{:S(2)}) copy-start(bf16[768,2048]{1,0:T(8,128)(2,1)} %get-tuple-element.92) | copy-start | bytes 9437188
  194.4 5.2 %copy-start.10 = (bf16[512,2048]{1,0:T(8,128)(2,1)S(1)}, bf16[512,2048]{1,0:T(8,128)(2,1)}, u32[]{:S(2)}) copy-start(bf16[512,2048]{1,0:T(8,128)(2,1)} %get-tuple-element.171.refs_0_) | copy-start | bytes 6291460
  207.3 7.5 %copy-start.14 = (bf16[512,768]{0,1:T(8,128)(2,1)}, bf16[512,768]{0,1:T(8,128)(2,1)S(1)}, u32[]{:S(2)}) copy-start(bf16[512,768]{0,1:T(8,128)(2,1)S(1)} %fusion.35) | copy-start | bytes 2359300
  207.3 2.0 copy-start.61
  208.4 10.6 %copy-start.16 = (bf16[512,768]{1,0:T(8,128)(2,1)}, bf16[512,768]{1,0:T(8,128)(2,1)S(1)}, u32[]{:S(2)}) copy-start(bf16[512,768]{1,0:T(8,128)(2,1)S(1)} %fusion.23.refs_13_) | copy-start | bytes 2359300
  210.6 2.0 copy-start.60
  213.9 2.0 copy-start.59
  215.9 2.3 copy-start.42
  302.6 4.4 %copy-start.26 = (bf16[768,640]{1,0:T(8,128)(2,1)S(1)}, bf16[768,640]{1,0:T(8,128)(2,1)}, u32[]{:S(2)}) copy-start(bf16[768,640]{1,0:T(8,128)(2,1)} %get-tuple-element.107) | copy-start | bytes 2949124
  302.6 4.4 %copy-start.38 = (bf16[512,640]{1,0:T(8,128)(2,1)S(1)}, bf16[512,640]{1,0:T(8,128)(2,1)}, u32[]{:S(2)}) copy-start(bf16[512,640]{1,0:T(8,128)(2,1)} %get-tuple-element.106) | copy-start | bytes 1966084
  314.1 2.7 copy-start.11
  314.1 2.7 copy-start.13
  315.7 1.9 copy-start.2
  (31 other events, 42.7 us)

commit v3 on v2

--- a/solution.py
+++ b/solution.py
@@ -993,14 +993,14 @@
 def attend_back_body(layout, *refs):
     grad_out, packed, lse, attended, cosine, sine, seg_row, seg_col, left_up, left_down = refs[:10]
     ups, downs = refs[10:14], refs[14:18]
-    p0, p1, p2, p3, r0, r1, r2, r3, summed, square_out = refs[18:28]
-    grads, leaving, keys_t, probs, prob_grads, found, going, coming = refs[28:36]
-    send_sem, recv_sem, out_send, out_recv = refs[36:40]
+    r0, r1, r2, r3, summed, square_out = refs[18:24]
+    grads, leaving, keys_t, probs, prob_grads, found, going, coming = refs[24:32]
+    send_sem, recv_sem, out_send, out_recv = refs[32:36]
     span = ups[0].shape[1]
     outs = [summed.at[:, pl.ds(0, span)], summed.at[:, pl.ds(span, span)]]
     wide_refs = [[(ups, 0, span)], [(downs, 0, span)]]
     start_loads, begin, advance, turns, finish, drain = reduce_tools(
-        layout, None, None, None, None, (left_up, left_down), wide_refs, outs, refs[40:]
+        layout, None, None, None, None, (left_up, left_down), wide_refs, outs, refs[36:]
     )
     start_loads()
     device = neighbours()["c"]
@@ -1022,8 +1022,7 @@
         crossing(place).start()
         grads[place, pl.ds(0, rows), 0:64] = grad_out[:, 64 * place : 64 * place + 64]
     nothing = jnp.zeros((rows, 64), jnp.bfloat16)
-    for order, (part, right) in enumerate(((p0, r0), (p2, r2), (p1, r1), (p3, r3))):
-        part[:, 576:640] = nothing
+    for order, right in enumerate((r0, r2, r1, r3)):
         right[:, 576:640] = nothing
         right[:, 640:832] = attended[:, 192 * order : 192 * order + 192]
         right[:, 832:896] = nothing
@@ -1096,7 +1095,7 @@
                 place = 3 * side + head
                 pair = turn_halves(found[place, at, 0:128], cosine[at], -sine[at]).astype(jnp.bfloat16)
                 value = found[place, at, 128:192].astype(jnp.bfloat16)
-                puts = [going.at[side]] if half else [(p0, p2)[side], (r0, r2)[side]]
+                puts = [going.at[side]] if half else [(r0, r2)[side]]
                 for put in puts:
                     put[:, 192 * head : 192 * head + 128] = pair
                     put[:, 192 * head + 128 : 192 * head + 192] = value
@@ -1105,8 +1104,7 @@
     square_out[...] = jnp.full(square_out.shape, finish(), jnp.float32)
     for side in range(2):
         returning(side).wait_recv()
-        for put in ((p1, p3)[side], (r1, r3)[side]):
-            put[:, 0:576] = coming[side, :, 0:576]
+        (r1, r3)[side][:, 0:576] = coming[side, :, 0:576]
     for place in range(6):
         crossing(place).wait_send()
     for side in range(2):
@@ -1122,14 +1120,13 @@
     found = pl.pallas_call(
         functools.partial(attend_back_body, layout),
         name="attend_back",
-        out_shape=[jax.ShapeDtypeStruct((rows, 640), jnp.bfloat16)] * 4
-        + [jax.ShapeDtypeStruct((rows, 896), jnp.bfloat16)] * 4
+        out_shape=[jax.ShapeDtypeStruct((rows, 896), jnp.bfloat16)] * 4
         + [
             jax.ShapeDtypeStruct((lefts[0].shape[0] // lax.axis_size("dp"), width), jnp.float32),
             jax.ShapeDtypeStruct((8, 128), jnp.float32),
         ],
         in_specs=[inside] * 10 + [anywhere] * 8,
-        out_specs=[inside] * 10,
+        out_specs=[inside] * 6,
         scratch_shapes=[
             pltpu.VMEM((6, 2 * rows, 128), jnp.bfloat16),
             pltpu.VMEM((6, rows, 128), jnp.bfloat16),
@@ -1149,7 +1146,7 @@
             collective_id=3, has_side_effects=True, vmem_limit_bytes=62 << 20
         ),
     )(grad_out, packed, lse, attended, cosine, sine, seg_row, seg_col, *lefts, *ups, *downs)
-    return found[:4], found[4:8], found[8], found[9]
+    return [item[:, :640] for item in found[:4]], found[:4], found[4], found[5]
 
 
 def pieces_of(width):

time: 442 us -> 442 us (level)
    unnamed x127 -> x125, local copies, waits for them, and re-layouts: 14.1 us -> 13.5 us
where the time goes in v3:
time: 442 us; the launch traced here: 436 us
  Pallas kernels  321 us (73%)
  matrix products  49.8 us (11%)
  other arithmetic  37.8 us (9%)
  local copies, waits for them, and re-layouts  23.3 us (5%)
    pallas_call x1, Pallas kernels, start_kernel(): pl.pallas_call(functools.partial(start_body, items), name='start', out_sh...  132 us
    pallas_call x1, Pallas kernels, reduce_kernel(): pl.pallas_call(functools.partial(reduce_body, layout, parts, gains_at), n...  107 us
    pallas_call x1, Pallas kernels, attend_back_kernel(): pl.pallas_call(functools.partial(attend_back_body, layout), name='attend_...  76.1 us
    dot_general x17, matrix products, mm_nt(): lax.dot_general(left, right, (((1,), (1,)), ((), ())), preferred_element_...  26.7 us
    dot_general x13, matrix products, mm(): return jnp.dot(left, right, preferred_element_type=jnp.float32)  23.1 us
    unnamed x125, local copies, waits for them, and re-layouts  13.5 us
    convert_element_type x7, other arithmetic, narrow(): return value.astype(jnp.bfloat16)  11 us

profile of v3, /device:TPU:0, one launch (start us, length us, event | category | flops | bytes accessed | tf_op | source)
XLA Modules:
  0.0 435.7 jit_solution(13547624302631946412)
XLA Ops:
  0.7 2.0 convert_bitcast_fusion.2.refs_0_
  12.1 1.9 fusion.34
  18.1 132.2 %start.1 = (bf16[768,2048]{1,0:T(8,128)(2,1)}, bf16[768,2048]{1,0:T(8,128)(2,1)}, bf16[768,2048]{1,0:T(8,128)(2,1)}, bf16[768,2048]{1,0:T(8,128)(2,1)}, bf16[768...) custom-call(bf16[96,2048]{1,0:T(8,128)(2,1)} %convert_bitcast_fusion, ...), custom_call_target="tpu_custom_call" | custom-call | tf_op jit(solution)/shard_map/start/pallas_call | solution.py:405
  150.3 2.0 copy.147
  152.4 2.5 multiply_reduce_fusion.8
  157.2 2.1 multiply_convert_fusion.6
  159.3 2.1 multiply_convert_fusion.7
  163.0 2.1 multiply_convert_fusion.9
  166.6 2.1 multiply_convert_fusion.8
  172.7 2.0 fusion.44
  174.7 2.2 fusion.47
  176.9 2.0 fusion.45
  178.9 2.0 fusion.46
  180.9 5.0 %select_reduce_fusion.2 = (f32[512]{0:T(512)S(1)}, f32[512]{0:T(512)S(1)}, f32[512]{0:T(512)S(1)}, f32[512]{0:T(512)S(1)}, f32[512]{0:T(512)S(1)}, /*index=5*/f32[512]{0:T(512)S(1)}, f32[512]{0:T(512)S(1)}, f32[512]{0:T(512)S(1)}) fusion(f32[512,2048]{1,0:T(8,128)S(1)} %get-tuple-element.189, s32[512]{0:T(512)S(1)} %get-tuple-element.150, ...), kind=kLoop, calls=%fused_computation.2 | loop fusion | flops 20967424 | bytes 16803840 | tf_op jit(solution)/shard_map/reduce_sum | solution.py:1437
  186.5 7.9 %multiply_convert_fusion = (bf16[512,2048]{1,0:T(8,128)(2,1)S(1)}, bf16[512,2048]{1,0:T(8,128)(2,1)}, bf16[512,2048]{1,0:T(8,128)(2,1)}, bf16[512,2048]{1,0:T(8,128)(2,1)}) fusion(f32[512,2048]{1,0:T(8,128)S(1)} %get-tuple-element.183, s32[512]{0:T(512)S(1)} %get-tuple-element.153, f32[512]{0:T(512)S(1)} %get-tuple-element.147, ...), kind=kLoop, calls=%fused_computation.4 | loop fusion | flops 25165824 | bytes 25178112 | tf_op jit(solution)/shard_map/convert_element_type | solution.py:1193
  194.4 5.1 %fusion.53 = f32[512,768]{0,1:T(8,128)S(1)} fusion(bf16[512,2048]{1,0:T(8,128)(2,1)} %get-tuple-element.162.refs_1_, bf16[768,2048]{1,0:T(8,128)(2,1)} %get-tuple-element.90), kind=kOutput, calls=%fused_computation.151 | convolution fusion | flops 1610612736 | bytes 6815744 | tf_op jit(solution)/shard_map/dot_general | solution.py:1233
  199.6 1.8 fusion.51
  201.4 1.8 fusion.52
  203.2 2.3 multiply_reduce_fusion.1
  216.0 1.4 fusion.11.refs_12_
  219.5 1.3 multiply_reduce_fusion.2
  220.9 1.7 convert_bitcast_fusion.1
  222.5 1.8 convolution_convert_fusion.refs_0_
  225.5 76.1 %attend_back.1 = (bf16[512,896]{1,0:T(8,128)(2,1)}, bf16[512,896]{1,0:T(8,128)(2,1)}, bf16[512,896]{1,0:T(8,128)(2,1)}, bf16[512,896]{1,0:T(8,128)(2,1)}, f32[96,1536]{1,0:T(8,128)}, /*index=5*/f32[8,128]{1,0:T(8,128)}) custom-call(bf16[512,768]{1,0:T(8,128)(2,1)} %convolution_convert_fusion.refs_0_, bf16[6,1024,256]{2,1,0:T(8,128)(2,1)} %get-tuple-element.92.refs_1_, ...), custom_call_target="tpu_custom_call" | custom-call | tf_op jit(solution)/shard_map/attend_back/pallas_call | solution.py:1120
  302.3 2.0 select_add_fusion.refs_8_
  304.3 1.6 multiply_reduce_fusion.4
  305.9 2.1 fusion.26
  311.3 2.3 multiply_reduce_fusion
  313.8 1.6 pad.9.refs_10_
  317.3 1.4 fusion.24.refs_12_
  319.9 107.0 %reduce_grads.1 = (f32[96,2048]{1,0:T(8,128)}, f32[96,896]{1,0:T(8,128)}, f32[8,128]{1,0:T(8,128)}) custom-call(bf16[512,2048]{1,0:T(8,128)(2,1)} %get-tuple-element.163.refs_0_, bf16[512,2048]{1,0:T(8,128)(2,1)} %get-tuple-element.162.refs_1_, bf16[512,2048]{1,0:T(8,128)(2,1)} %get-tuple-element.161.refs_2_, bf16[512,2048]{1,0:T(8,128)(2,1)} %copy-done.8, ...), custom_call_target="tpu_custom_call" | custom-call | tf_op jit(solution)/shard_map/reduce_grads/pallas_call | solution.py:819
  428.4 5.8 %update_weights.1 = (f32[96,2048]{1,0:T(8,128)}, f32[96,2048]{1,0:T(8,128)}, f32[96,2048]{1,0:T(8,128)}, f32[96,576]{1,0:T(8,128)}, f32[96,576]{1,0:T(8,128)}, /...) custom-call(f32[8,128]{1,0:T(8,128)} %get-tuple-element.103.refs_0_,, ...), custom_call_target="tpu_custom_call" | custom-call | tf_op jit(solution)/shard_map/update_weights/pallas_call | solution.py:888
  (188 shorter events, 45.1 us)
Async XLA Ops:
  0.7 4.5 %copy-start.22 = (f32[96,768]{1,0:T(8,128)S(1)}, f32[96,768]{1,0:T(8,128)}, u32[]{:S(2)}) copy-start(f32[96,768]{1,0:T(8,128)} %refs_14_.1) | copy-start | bytes 884740
  0.7 5.2 %copy-start.23 = (f32[768,96]{0,1:T(8,128)S(1)}, f32[768,96]{0,1:T(8,128)}, u32[]{:S(2)}) copy-start(f32[768,96]{0,1:T(8,128)} %param.32) | copy-start | bytes 884740
  0.7 5.9 %copy-start.38 = (f32[192,96]{1,0:T(8,128)S(1)}, f32[192,96]{1,0:T(8,128)}, u32[]{:S(2)}) copy-start(f32[192,96]{1,0:T(8,128)} %refs_11_.1) | copy-start | bytes 221188
  0.7 6.6 %copy-start.39 = (s32[2,4]{1,0:T(2,128)S(1)}, s32[2,4]{1,0:T(2,128)}, u32[]{:S(2)}) copy-start(s32[2,4]{1,0:T(2,128)} %param.24) | copy-start | bytes 100
  0.7 6.9 %copy-start.57 = (s32[2]{0:T(128)S(1)}, s32[2]{0:T(128)}, u32[]{:S(2)}) copy-start(s32[2]{0:T(128)} %param.25) | copy-start | bytes 28
  150.3 2.0 copy-start.30
  150.3 2.0 copy-start.52
  150.3 2.0 copy-start.53
  152.3 2.6 copy-start
  157.2 2.1 copy-start.48
  159.3 11.1 %copy-start.15 = (bf16[512,768]{1,0:T(8,128)(2,1)}, bf16[512,768]{1,0:T(8,128)(2,1)S(1)}, u32[]{:S(2)}) copy-start(bf16[512,768]{1,0:T(8,128)(2,1)S(1)} %get-tuple-element.178.refs_17_) | copy-start | bytes 2359300
  159.3 2.1 copy-start.50
  163.0 2.1 copy-start.46
  166.6 2.9 copy-start.42
  172.7 2.0 copy-start.4
  174.7 2.2 copy-start.7
  176.9 2.0 copy-start.5
  194.4 8.9 %copy-start.8 = (bf16[512,2048]{1,0:T(8,128)(2,1)}, bf16[512,2048]{1,0:T(8,128)(2,1)S(1)}, u32[]{:S(2)}) copy-start(bf16[512,2048]{1,0:T(8,128)(2,1)S(1)} %get-tuple-element.160.refs_3_) | copy-start | bytes 6291460
  194.4 5.2 %copy-start.6 = (bf16[768,2048]{1,0:T(8,128)(2,1)S(1)}, bf16[768,2048]{1,0:T(8,128)(2,1)}, u32[]{:S(2)}) copy-start(bf16[768,2048]{1,0:T(8,128)(2,1)} %get-tuple-element.88) | copy-start | bytes 9437188
  194.4 5.2 %copy-start.10 = (bf16[512,2048]{1,0:T(8,128)(2,1)S(1)}, bf16[512,2048]{1,0:T(8,128)(2,1)}, u32[]{:S(2)}) copy-start(bf16[512,2048]{1,0:T(8,128)(2,1)} %get-tuple-element.163.refs_0_) | copy-start | bytes 6291460
  207.3 7.5 %copy-start.14 = (bf16[512,768]{0,1:T(8,128)(2,1)}, bf16[512,768]{0,1:T(8,128)(2,1)S(1)}, u32[]{:S(2)}) copy-start(bf16[512,768]{0,1:T(8,128)(2,1)S(1)} %fusion.42) | copy-start | bytes 2359300
  207.3 2.0 copy-start.60
  208.4 10.6 %copy-start.16 = (bf16[512,768]{1,0:T(8,128)(2,1)}, bf16[512,768]{1,0:T(8,128)(2,1)S(1)}, u32[]{:S(2)}) copy-start(bf16[512,768]{1,0:T(8,128)(2,1)S(1)} %fusion.23.refs_13_) | copy-start | bytes 2359300
  210.6 2.0 copy-start.59
  213.9 2.0 copy-start.58
  216.0 2.3 copy-start.41
  301.6 4.3 copy-start.19
  305.9 2.2 copy-start.18
  305.9 2.2 copy-start.21
  308.1 2.3 copy-start.28
  313.8 2.7 copy-start.11
  313.8 2.7 copy-start.13
  (30 other events, 42.3 us)
